TPU v7x, 128 devices: a whole 4x4x4 slice. The times are simulated.
128 devices in a mesh: block: 8 (over y, core), node: 16 (over x, z).
Axes of the slice: x: 4, y: 4, z: 4, core: 2. Of those that a mesh axis runs over, the one named last changes fastest.
Arguments:
- vectors: float32 [8, 32768, 512], P('block', 'node'), may hold values from -6 to 6
- col_factors: float32 [8, 5, 512, 64, 128], P('block', None, 'node'), may hold values from -0.625 to 0.625
- row_factors: float32 [8, 4, 512, 64, 128], P('block', None, 'node'), may hold values from -0.625 to 0.625
- col_ranks: int32 [8, 5, 512], P('block', None, 'node'), may hold values from 16 to 64, as said below
- row_ranks: int32 [8, 4, 512], P('block', None, 'node'), may hold values from 16 to 64, as said below
- row_weights: float32 [32768], P('node'), may hold values from 0.05 to 0.5
Outputs:
- block_row: float32 [32768, 512], P('node')
- transposed: float32 [8, 32768, 512], P('block', 'node')
Inputs may be any that keep to these rules, and one draw needn't show every extreme that they name: `col_ranks`: every rank is at least a quarter of 64; in each block and level the first span has rank 64. `row_ranks`: every rank is at least a quarter of 64; in each block and level the first span in row order has rank 64.
All inputs are finite; a program needn't handle non-finite values.
Results may differ from a plain program's by a relative error of at most 0.0001.
Values sent between devices are 32-bit elements; how exact they have to be, the bound alone decides.
No kernel may reach another device: no remote copies, remote signals or barrier semaphores. Data moves between devices by JAX's collectives and lax.ppermute only.
A program may use at most 128 MiB of HBM per device.

v0:
```python
import functools
import jax
import jax.numpy as jnp
from jax import lax
from jax.experimental import pallas as pl
from jax.experimental.pallas import tpu as pltpu
from jax.sharding import PartitionSpec as P


CHUNKS = 2
SUB = 2
F32 = jnp.float32
BF16 = jnp.bfloat16
PARAMS = pltpu.CompilerParams(vmem_limit_bytes=67043328)


def split(value):
    high = value.astype(jnp.bfloat16)
    low = (value - high.astype(F32)).astype(jnp.bfloat16)
    return high, low


def pair_of(j, bit):
    first = ((j >> bit) << (bit + 1)) + (j & ((1 << bit) - 1))
    return first, first + (1 << bit)


def level_pass(load, store, f_ref, ranks, level, bit, back):
    span = f_ref.shape[-2]
    row_ids = lax.broadcasted_iota(jnp.int32, (span, 2 * span), 0)
    for j in range(f_ref.shape[-3] // 2):
        pair = pair_of(j, bit)
        factor = jnp.concatenate([jnp.where(row_ids < ranks[level, 0, c], f_ref[0, c], 0.0) for c in pair], axis=0)
        if back:
            factor = factor.T
        f_high, f_low = split(factor)
        lhs = jnp.concatenate([f_high, f_low], axis=0)
        lhs = jnp.concatenate([lhs, lhs], axis=1)
        x_high, x_low = split(jnp.concatenate([load(c) for c in pair], axis=0))
        rhs = jnp.concatenate([x_high, x_low], axis=0)
        out = jnp.dot(lhs, rhs, preferred_element_type=F32)
        out = out[: 2 * span] + out[2 * span :]
        store(pair, out[:span], out[span:])


def reader(ref, span):
    return lambda c: ref[c * span : (c + 1) * span, :]


def writer(ref, span):
    def store(spans, *values):
        for c, value in zip(spans, values):
            ref[c * span : (c + 1) * span, :] = value

    return store


def run_levels(levels, first_bit, back, ranks, f_ref, load, store, bufs):
    span = f_ref.shape[-2]
    for s in range(levels):
        level = levels - 1 - s if back else s
        src = load if s == 0 else reader(bufs[(s - 1) % 2], span)
        dst = store if s == levels - 1 else writer(bufs[s % 2], span)

        @pl.when(pl.program_id(0) == s)
        def _(src=src, dst=dst, level=level):
            level_pass(src, dst, f_ref, ranks, level, first_bit + level, back)


def cost(rows, columns, levels):
    return pl.CostEstimate(
        flops=levels * 16 * rows * 128 * columns, transcendentals=0, bytes_accessed=levels * (1 << 20) + 8 * rows * columns
    )


def factor_spec(factors, back):
    levels = factors.shape[1]
    return pl.BlockSpec((None, 1) + factors.shape[2:], lambda s: (0, levels - 1 - s if back else s, 0, 0, 0))


def whole(shape, chunk=0):
    return pl.BlockSpec(shape, lambda s: (0, chunk))


SMEM = pl.BlockSpec(memory_space=pltpu.SMEM)


def column_kernel(levels, back, ranks, x_ref, f_ref, o_ref, buf_a, buf_b):
    span = f_ref.shape[-2]
    run_levels(levels, 0, back, ranks, f_ref, reader(x_ref, span), writer(o_ref, span), [buf_a, buf_b])


def column_tree(x, factors, ranks, columns, chunk):
    levels, rows = factors.shape[1], x.shape[0]
    return pl.pallas_call(
        functools.partial(column_kernel, levels, False),
        grid=(levels,),
        out_shape=jax.ShapeDtypeStruct((rows, columns), F32),
        in_specs=[SMEM, whole((rows, columns), chunk), factor_spec(factors, False)],
        out_specs=whole((rows, columns)),
        scratch_shapes=[pltpu.VMEM((rows, columns), F32)] * 2,
        compiler_params=PARAMS,
        cost_estimate=cost(rows, columns, levels),
        name="column_tree",
    )(ranks, x, factors)


def quad_of(j, bit):
    base = ((j >> bit) << (bit + 2)) + (j & ((1 << bit) - 1))
    return [base + (n << bit) for n in range(4)]


def three(high, low, axis):
    return jnp.concatenate([high, high, low] if axis == 1 else [high, low, high], axis=axis)


def merge_kernel(first_bit, ranks, fa_ref, fb_ref, *refs):
    g_ref, t_ref = refs[-2:]
    span = fa_ref.shape[-2]
    lane = lax.broadcasted_iota(jnp.int32, (2 * span, 2 * span), 1)
    row_ids = lax.broadcasted_iota(jnp.int32, (span, 2 * span), 0)
    for s in range(2):

        @pl.when(pl.program_id(0) == s)
        def _(s=s):
            bit = first_bit + 2 * s
            masked = lambda ref, level, c: jnp.where(row_ids < ranks[level, 0, c], ref[0, c], 0.0)
            for j in range(g_ref.shape[1]):
                quad = quad_of(j, bit)
                rows = [None] * 4
                for a in range(2):
                    spans = (quad[a], quad[2 + a])
                    inner = jnp.concatenate([masked(fa_ref, 2 * s, c) for c in spans], axis=0)
                    outer = jnp.concatenate([masked(fb_ref, 2 * s + 1, c) for c in spans], axis=0)
                    outer = jnp.concatenate([jnp.where(lane < span, outer, 0.0), jnp.where(lane < span, 0.0, outer)], axis=0)
                    both = jnp.dot(three(*split(outer), 1), three(*split(inner), 0), preferred_element_type=F32)
                    both = jnp.concatenate([both[: 2 * span], both[2 * span :]], axis=1)
                    rows[a], rows[2 + a] = both[:span], both[span:]
                merged = jnp.concatenate(rows, axis=0)
                for out, value in ((g_ref, merged), (t_ref, merged.T)):
                    high, low = split(value)
                    out[0, j, 0] = high
                    out[0, j, 1] = low


def merge_columns_kernel(first_bit, last, ranks, fa_ref, fb_ref, fe_ref, w_ref, v_ref, g_ref, t_ref):
    span = fa_ref.shape[-2]
    row_ids = lax.broadcasted_iota(jnp.int32, (span, 2 * span), 0)

    @pl.when(pl.program_id(0) == 0)
    def _():
        for j in range(w_ref.shape[0]):
            pair = pair_of(j, last)
            factor = jnp.concatenate([jnp.where(row_ids < ranks[last, 0, c], fe_ref[0, c], 0.0) for c in pair], axis=0)
            w_ref[j] = jnp.concatenate(split(factor), axis=0)
            v_ref[j] = jnp.concatenate(split(factor.T), axis=0)

    merge_kernel(first_bit, ranks, fa_ref, fb_ref, g_ref, t_ref)


def merge_rows_kernel(first_bit, ranks, fa_ref, fb_ref, weight_ref, b_ref, g_ref, t_ref):
    @pl.when(pl.program_id(0) == 0)
    def _():
        size = weight_ref.shape[1]
        for n in range(weight_ref.shape[0]):
            b_ref[n * size : (n + 1) * size, :] = jnp.broadcast_to(weight_ref[n : n + 1, :], (size, size)).T

    merge_kernel(first_bit, ranks, fa_ref, fb_ref, g_ref, t_ref)


def level_spec(factors, index):
    return pl.BlockSpec((None, 1) + factors.shape[2:], lambda s: (0, index(s), 0, 0, 0))


def merged_shapes(factors):
    quads, side = factors.shape[2] // 4, 4 * factors.shape[3]
    shape = jax.ShapeDtypeStruct((2, quads, 2, side, side), BF16)
    return shape, pl.BlockSpec((1, quads, 2, side, side), lambda s: (s, 0, 0, 0, 0))


def merge_columns(factors, ranks):
    shape, spec = merged_shapes(factors)
    last = factors.shape[1] - 1
    pairs, width = factors.shape[2] // 2, 2 * factors.shape[3]
    single = jax.ShapeDtypeStruct((pairs, 2 * width, width), BF16)
    single_spec = pl.BlockSpec(single.shape, lambda s: (0, 0, 0))
    return pl.pallas_call(
        functools.partial(merge_columns_kernel, 0, last),
        grid=(2,),
        out_shape=(single, single, shape, shape),
        in_specs=[SMEM]
        + [level_spec(factors, f) for f in (lambda s: 2 * s, lambda s: 2 * s + 1, lambda s: last)],
        out_specs=(single_spec, single_spec, spec, spec),
        compiler_params=PARAMS,
        cost_estimate=pl.CostEstimate(flops=10**10, transcendentals=0, bytes_accessed=15 << 20),
        name="merge_columns",
    )(ranks, factors, factors, factors)


def merge_rows(factors, ranks, weights, first_bit):
    shape, spec = merged_shapes(factors)
    weights = weights.reshape(-1, 128)
    rows = weights.size
    return pl.pallas_call(
        functools.partial(merge_rows_kernel, first_bit),
        grid=(2,),
        out_shape=(jax.ShapeDtypeStruct((rows, 128), F32), shape, shape),
        in_specs=[SMEM] + [level_spec(factors, f) for f in (lambda s: 2 * s, lambda s: 2 * s + 1)] + [whole2(weights.shape)],
        out_specs=(whole2((rows, 128)), spec, spec),
        compiler_params=PARAMS,
        cost_estimate=pl.CostEstimate(flops=10**10, transcendentals=0, bytes_accessed=12 << 20),
        name="merge_rows",
    )(ranks, factors, factors, weights)


def whole2(shape):
    return pl.BlockSpec(shape, lambda s: (0, 0))


def spans_of(ref, span, bit, sub, streamed):
    def rows(q, n, count):
        if streamed and len(ref.shape) == 4:
            return (n, 0, slice(q * span, (q + 1) * span), slice(None))
        group = quad_of if count == 4 else pair_of
        if streamed:
            c = group(q, bit)[n]
            return (slice(c * span, (c + 1) * span), slice(None))
        total = ref.shape[0] // span // count // SUB
        return (pl.ds(pl.multiple_of(group(sub * total + q, bit)[n] * span, span), span), slice(None))

    def load(q, count):
        return jnp.concatenate([ref[rows(q, n, count)] for n in range(count)], axis=0)

    def store(q, values):
        for n, value in enumerate(values):
            ref[rows(q, n, len(values))] = value

    return load, store


def quad_pass(load, store, g_ref):
    for q in range(g_ref.shape[0]):
        x = load(q, 4)
        out = jnp.dot(three(g_ref[q, 0], g_ref[q, 1], 1), three(*split(x), 0), preferred_element_type=F32)
        size = out.shape[0] // 4
        store(q, [out[n * size : (n + 1) * size] for n in range(4)])


def pair_pass(load, store, w_ref):
    for q in range(w_ref.shape[0]):
        x = load(q, 2)
        lhs = jnp.concatenate([w_ref[q], w_ref[q]], axis=1)
        out = jnp.dot(lhs, jnp.concatenate(split(x), axis=0), preferred_element_type=F32)
        size = out.shape[0] // 4
        out = out[: 2 * size] + out[2 * size :]
        store(q, [out[:size], out[size:]])


def run_stages(stages, x_ref, o_ref, bufs, span):
    for s, (bit, stage) in enumerate(stages):
        first, last = s == 0, s == len(stages) - 1

        @pl.when(pl.program_id(0) // SUB == s)
        def _(s=s, bit=bit, stage=stage, first=first, last=last):
            sub = lax.rem(pl.program_id(0), SUB)
            if callable(x_ref) and first:
                load = x_ref(sub, bit)
            else:
                load = spans_of(x_ref if first else bufs[(s - 1) % 2], span, bit, sub, first)[0]
            if callable(o_ref) and last:
                store = o_ref
            else:
                store = spans_of(o_ref if last else bufs[s % 2], span, bit, sub, last)[1]
            stage(load, store)


def part(step, stage):
    return jnp.clip(step - stage * SUB, 0, SUB - 1)


def merged_spec(merged, first, back):
    quads = merged.shape[1] // SUB

    def index(step):
        at = jnp.clip(step - first * SUB, 0, 2 * SUB - 1)
        stage = at // SUB
        return (1 - stage if back else stage, lax.rem(at, SUB), 0, 0, 0)

    return pl.BlockSpec((None, quads) + merged.shape[2:], index)


def merged_column_kernel(back, last, x_ref, w_ref, g_ref, *rest):
    o_ref, buf_a, buf_b = rest[-3:]
    span = w_ref.shape[-1] // 2
    quads = lambda load, store: quad_pass(load, store, g_ref)
    stages = [(0, quads), (2, quads), (last, lambda load, store: pair_pass(load, store, w_ref))]
    run_stages(stages[::-1] if back else stages, x_ref, o_ref, [buf_a, buf_b], span)


def merged_columns(x, single, merged, back, columns, chunk=0, into=None, out_chunk=0, total=None, after=()):
    rows = x.shape[0]
    extra = list(after) if into is None else [into] + list(after)
    size = single.shape[0] // SUB * 64
    w_spec = pl.BlockSpec((size // 64,) + single.shape[1:], lambda s: (part(s, 0 if back else 2), 0, 0))
    if back:
        x = x.reshape(2, SUB, size, columns)
        x_spec = pl.BlockSpec((2, 1, size, columns), lambda s: (0, part(s, 0), 0, 0))
        out_shape = (rows, total)
        o_spec = pl.BlockSpec((rows // SUB, columns), lambda s: (part(s, 2), out_chunk))
    else:
        x_spec = pl.BlockSpec((rows // SUB, columns), lambda s: (part(s, 0), chunk))
        out_shape = (2, SUB, size, columns)
        o_spec = pl.BlockSpec((2, 1, size, columns), lambda s: (0, part(s, 2), 0, 0))
    out = pl.pallas_call(
        functools.partial(merged_column_kernel, back, 4),
        grid=(3 * SUB,),
        out_shape=jax.ShapeDtypeStruct(out_shape, F32),
        in_specs=[x_spec, w_spec, merged_spec(merged, 1 if back else 0, back)] + [pl.BlockSpec(memory_space=pl.ANY)] * len(extra),
        out_specs=o_spec,
        scratch_shapes=[pltpu.VMEM((rows, columns), F32)] * 2,
        input_output_aliases={} if into is None else {3: 0},
        compiler_params=PARAMS,
        cost_estimate=pl.CostEstimate(flops=4 * 10**9, transcendentals=0, bytes_accessed=9 << 20),
        name="column_back" if back else "column_tree_merged",
    )(x, single, merged, *extra)
    return out if back else out.reshape(rows, columns)


def row_kernel(first_bit, span, place, x_ref, g_ref, keep_ref, send_ref, buf):
    swap = place[1] == 1

    def store(q, values):
        at = slice(q * span, (q + 1) * span)
        for n in range(2):
            keep_ref[n, 0, at, :] = jnp.where(swap, values[n + 2], values[n])
            send_ref[n, 0, at, :] = jnp.where(swap, values[n], values[n + 2])

    quads = lambda load, put: quad_pass(load, put, g_ref)
    run_stages([(first_bit, quads), (first_bit + 2, quads)], x_ref, store, [buf], span)


def row_tree(x, merged, place, first_bit, span):
    rows, columns = x.shape
    size = rows // 4 // SUB
    half = jax.ShapeDtypeStruct((2, SUB, size, columns), F32)
    half_spec = pl.BlockSpec((2, 1, size, columns), lambda s: (0, part(s, 1), 0, 0))
    keep, send = pl.pallas_call(
        functools.partial(row_kernel, first_bit, span),
        grid=(2 * SUB,),
        out_shape=(half, half),
        in_specs=[SMEM, pl.BlockSpec((rows // SUB, columns), lambda s: (part(s, 0), 0)), merged_spec(merged, 0, False)],
        out_specs=(half_spec, half_spec),
        scratch_shapes=[pltpu.VMEM((rows, columns), F32)],
        compiler_params=PARAMS,
        cost_estimate=pl.CostEstimate(flops=3 * 10**9, transcendentals=0, bytes_accessed=8 << 20),
        name="row_tree",
    )(place, x, merged)
    return keep.reshape(rows // 2, columns), send.reshape(rows // 2, columns)


def add_halves_kernel(ring, place, keep_ref, got_ref, *refs):
    outs, (k_buf, g_buf, in_sems, out_sems) = refs[:ring], refs[ring:]
    size = outs[0].shape[0]
    copies = []
    for d in range(ring):
        rows = pl.ds(pl.multiple_of(lax.rem(place[0] + d, ring) * size, size), size)
        copies.append(pltpu.make_async_copy(keep_ref.at[rows], k_buf.at[d], in_sems.at[0, d]))
        copies.append(pltpu.make_async_copy(got_ref.at[rows], g_buf.at[d], in_sems.at[1, d]))
    for copy in copies:
        copy.start()
    sends = []
    for d, out in enumerate(outs):
        copies[2 * d].wait()
        copies[2 * d + 1].wait()
        g_buf[d] = g_buf[d] + k_buf[d]
        sends.append(pltpu.make_async_copy(g_buf.at[d], out, out_sems.at[d]))
        sends[-1].start()
    for send in sends:
        send.wait()


HBM = pl.BlockSpec(memory_space=pltpu.HBM)


def add_halves(keep, got, place, ring):
    rows, columns = keep.shape
    size = rows // ring
    piece = jax.ShapeDtypeStruct((size, columns), F32)
    return pl.pallas_call(
        functools.partial(add_halves_kernel, ring),
        out_shape=(piece,) * ring,
        in_specs=[SMEM0, HBM, HBM],
        out_specs=(HBM,) * ring,
        scratch_shapes=[pltpu.VMEM((ring, size, columns), F32)] * 2
        + [pltpu.SemaphoreType.DMA((2, ring)), pltpu.SemaphoreType.DMA((ring,))],
        compiler_params=PARAMS,
        cost_estimate=pl.CostEstimate(flops=keep.size, transcendentals=0, bytes_accessed=12 * keep.size),
        name="add_halves",
    )(place, keep, got)


SMEM0 = pl.BlockSpec(memory_space=pltpu.SMEM)


def add_pieces_kernel(count, *refs):
    pieces, out = refs[:count], refs[count]
    buf, in_sems, out_sems = refs[count + 1 :]
    parts = buf.shape[1]
    size = out.shape[0] // parts
    copies = []
    for p in range(parts):
        for n, piece in enumerate(pieces):
            copies.append(pltpu.make_async_copy(piece.at[pl.ds(p * size, size)], buf.at[n, p], in_sems.at[n, p]))
            copies[-1].start()
    sends = []
    for p in range(parts):
        for n in range(count):
            copies[p * count + n].wait()
        total = buf[0, p]
        for n in range(1, count):
            total = total + buf[n, p]
        buf[0, p] = total
        sends.append(pltpu.make_async_copy(buf.at[0, p], out.at[pl.ds(p * size, size)], out_sems.at[p]))
        sends[-1].start()
    for send in sends:
        send.wait()


def add_pieces(pieces):
    rows, columns = pieces[0].shape
    count, parts = len(pieces), 2
    return pl.pallas_call(
        functools.partial(add_pieces_kernel, count),
        out_shape=jax.ShapeDtypeStruct((rows, columns), F32),
        in_specs=[HBM] * count,
        out_specs=HBM,
        scratch_shapes=[pltpu.VMEM((count, parts, rows // parts, columns), F32)]
        + [pltpu.SemaphoreType.DMA((count, parts)), pltpu.SemaphoreType.DMA((parts,))],
        compiler_params=PARAMS,
        cost_estimate=pl.CostEstimate(flops=4 * pieces[0].size, transcendentals=0, bytes_accessed=20 * pieces[0].size),
        name="add_pieces",
    )(*pieces)


def weigh_kernel(first_bit, span, ring, chunk, place, *refs):
    pieces = refs[: 2 * ring]
    w_ref, g_ref = refs[2 * ring : 2 * ring + 2]
    b_ref, o_ref, x_buf, buf, in_sems, out_sem = refs[-6:]
    size, columns = pieces[0].shape
    step = pl.program_id(0)
    out_copy = pltpu.make_async_copy(x_buf, b_ref.at[:, pl.ds(chunk * columns, columns)], out_sem)

    @pl.when(step == 0)
    def _():
        copies = []
        for n, piece in enumerate(pieces):
            side, d = divmod(n, ring)
            half = place[1] if side == 0 else 1 - place[1]
            start = half * (ring * size) + lax.rem(place[0] + ring - d, ring) * size
            rows = pl.ds(pl.multiple_of(start, size), size)
            copies.append(pltpu.make_async_copy(piece, x_buf.at[rows], in_sems.at[n]))
            copies[-1].start()
        for copy in copies:
            copy.wait()
        out_copy.start()

    def weighted(sub, bit):
        load, _ = spans_of(x_buf, span, bit, sub, False)
        load_weight, _ = spans_of(w_ref, span, bit, sub, False)

        def read(q, count):
            value, weight = load(q, count), load_weight(q, count)
            return value * jnp.concatenate([weight] * (value.shape[1] // weight.shape[1]), axis=1)

        return read

    quads = lambda load, store: quad_pass(load, store, g_ref)
    run_stages([(first_bit + 2, quads), (first_bit, quads)], weighted, o_ref, [buf], span)

    @pl.when(step == pl.num_programs(0) - 1)
    def _():
        out_copy.wait()


def weigh_back(pieces, weights, merged, place, first_bit, span, into, chunk, total, after=()):
    ring = len(pieces) // 2
    size, columns = pieces[0].shape
    rows = 2 * ring * size
    extra = list(after) if into is None else [into] + list(after)
    hbm = pl.BlockSpec(memory_space=pltpu.HBM)
    return pl.pallas_call(
        functools.partial(weigh_kernel, first_bit, span, ring, chunk),
        grid=(2 * SUB,),
        out_shape=(jax.ShapeDtypeStruct((rows, total), F32), jax.ShapeDtypeStruct((rows, columns), F32)),
        in_specs=[SMEM]
        + [hbm] * len(pieces)
        + [whole(weights.shape), merged_spec(merged, 0, True)]
        + [pl.BlockSpec(memory_space=pl.ANY)] * len(extra),
        out_specs=(hbm, pl.BlockSpec((rows // SUB, columns), lambda s: (part(s, 1), 0))),
        scratch_shapes=[pltpu.VMEM((rows, columns), F32)] * 2
        + [pltpu.SemaphoreType.DMA((len(pieces),)), pltpu.SemaphoreType.DMA],
        input_output_aliases={} if into is None else {3 + len(pieces): 0},
        compiler_params=PARAMS,
        cost_estimate=pl.CostEstimate(flops=3 * 10**9, transcendentals=0, bytes_accessed=12 << 20),
        name="weigh_back",
    )(place, *pieces, weights, merged, *extra)


def exchange(x):
    nodes = lax.axis_size("node")
    rows, columns = x.shape
    out = lax.all_to_all(x.reshape(nodes, rows // nodes, columns), "node", split_axis=0, concat_axis=0, tiled=True)
    return out.reshape(rows, columns)


def shards(vectors, col_factors, row_factors, col_ranks, row_ranks, row_weights):
    rows, total = vectors.shape[1:]
    columns = total // CHUNKS
    low_bits = col_factors.shape[1] - row_factors.shape[1]
    ring = lax.axis_size("block") // 2
    sibling = [(b, b ^ 1) for b in range(2 * ring)]
    shift = [[(b, (b + 2 * d) % (2 * ring)) for b in range(2 * ring)] for d in range(ring)]
    index = lax.axis_index("block")
    place = jnp.stack([index // 2, index % 2]).astype(jnp.int32)
    span = col_factors.shape[3]
    flat = vectors.reshape(rows, total)
    col_ranks = jnp.transpose(col_ranks, (1, 0, 2))
    row_ranks = jnp.transpose(row_ranks, (1, 0, 2))
    chunks = range(CHUNKS)
    t = column_tree(flat, col_factors, col_ranks, columns, 0)
    sent = [exchange(t)]
    single, single_back, col_merged, col_back = merge_columns(col_factors, col_ranks)
    weights, row_merged, row_back = merge_rows(row_factors, row_ranks, row_weights, low_bits)
    for n in chunks[1:]:
        t = merged_columns(flat, single, col_merged, False, columns, n, after=[weights])
        sent.append(exchange(t))
    halves = []
    for n in chunks:
        halves.append(row_tree(sent[n], row_merged, place, low_bits, span))

    def start(n):
        got = lax.ppermute(halves[n][1], "block", sibling)
        return add_halves(halves[n][0], got, place, ring)

    block_row = result = None
    back = []
    pieces = start(0)
    for n in chunks:
        later = n + 1 < CHUNKS
        got = [pieces[0]]
        for d in range(1, ring):
            got.append(lax.ppermute(pieces[d], "block", shift[d]))
        total_piece = add_pieces(got)
        mine = [total_piece]
        for d in range(1, ring):
            mine.append(lax.ppermute(total_piece, "block", shift[d]))
        if later:
            pieces = start(n + 1)
            mine[1:], pieces = lax.optimization_barrier((mine[1:], pieces))
        theirs = [lax.ppermute(piece, "block", sibling) for piece in mine]
        block_row, t = weigh_back(mine + theirs, weights, row_back, place, low_bits, span, block_row, n, total)
        back.append(exchange(t))
    for n in chunks:
        result = merged_columns(back[n], single_back, col_back, True, columns, 0, result, n, total)
    return block_row, result.reshape(1, rows, total)


def solution(mesh):
    in_specs = (
        P("block", "node", None),
        P("block", None, "node", None, None),
        P("block", None, "node", None, None),
        P("block", None, "node"),
        P("block", None, "node"),
        P("node"),
    )
    out_specs = (P("node", None), P("block", "node", None))
    return jax.shard_map(shards, mesh=mesh, in_specs=in_specs, out_specs=out_specs, check_vma=False)
```

profile of v0, /device:TPU:25, one launch (start us, length us, event | category | flops | bytes accessed | tf_op | source)
XLA Modules:
  0.0 227.3 jit_solution(14136426741664904002)
XLA Ops:
  0.6 8.1 %column_tree.1 = f32[2048,256]{1,0:T(8,128)} custom-call(s32[5,1,32]{2,1,0:T(1,128)} %bitcast.33, f32[2048,512]{1,0:T(8,128)} %bitcast.28, f32[1,5,32,64,128]{4,3,2,1,0:T(8,128)} %fe_ref.1), custom_call_target="tpu_custom_call" | custom-call | flops 5368709120 | bytes 9437184 | tf_op jit(solution)/shard_map/column_tree/pallas_call | solution.py:95
  8.7 7.7 %all-to-all-start = ((f32[16,128,256]{2,1,0:T(8,128)}), f32[16,128,256]{2,1,0:T(8,128)}, u32[]{:S(2)}, u32[]{:S(2)}) async-start(f32[16,128,256]{2,1,0:T(8,128)} %bitcast.25), calls=%async_computation | async-start | bytes 4194304 | tf_op jit(solution)/shard_map/all_to_all | solution.py:512
  16.3 7.8 %merge_columns.1 = (bf16[16,256,128]{2,1,0:T(8,128)(2,1)}, bf16[16,256,128]{2,1,0:T(8,128)(2,1)}, bf16[2,8,2,256,256]{4,3,2,1,0:T(8,128)(2,1)}, bf16[2,8,2,256,256]{4,3,2,1,0:T(8,128)(2,1)}) custom-call(s32[5,1,32]{2,1,0:T(1,128)} %bitcast.34, f32[1,5,32,64,128]{4,3,2,1,0:T(8,128)} %fe_ref.1, f32[1,5,32,64,128]{4,3,2,1,0:T(8,128)} %fe_ref.1, ...), custom_call_target="tpu_custom_call" | custom-call | flops 10000000000 | bytes 15728640 | tf_op jit(solution)/shard_map/merge_columns/pallas_call | solution.py:187
  24.2 7.2 %merge_rows.1 = (f32[2048,128]{1,0:T(8,128)}, bf16[2,8,2,256,256]{4,3,2,1,0:T(8,128)(2,1)}, bf16[2,8,2,256,256]{4,3,2,1,0:T(8,128)(2,1)}) custom-call(s32[4,1,32]{2,1,0:T(1,128)} %bitcast.35, f32[1,4,32,64,128]{4,3,2,1,0:T(8,128)} %fb_ref.2, f32[1,4,32,64,128]{4,3,2,1,0:T(8,128)} %fb_ref.2, f32[16,128]{1,0:T(8,128)} %bitcast.32), custom_call_target="tpu_custom_call" | custom-call | flops 10000000000 | bytes 12582912 | tf_op jit(solution)/shard_map/merge_rows/pallas_call | solution.py:204
  31.4 7.5 %column_tree_merged.1 = f32[2,2,512,256]{3,2,1,0:T(8,128)} custom-call(f32[2048,512]{1,0:T(8,128)} %bitcast.29, bf16[16,256,128]{2,1,0:T(8,128)(2,1)} %get-tuple-element.39.w_ref, bf16[2,8,2,256,256]{4,3,2,1,0:T(8,128)(2,1)} %get-tuple-element.40.g_ref, f32[2048,128]{1,0:T(8,128)} %get-tuple-element.41.rest_0_.refs_8_), custom_call_target="tpu_custom_call" | custom-call | flops 4000000000 | bytes 9437184 | tf_op jit(solution)/shard_map/column_tree_merged/pallas_call | solution.py:314
  38.9 5.6 %all-to-all-done = f32[16,128,256]{2,1,0:T(8,128)} async-done(((f32[16,128,256]{2,1,0:T(8,128)}), f32[16,128,256]{2,1,0:T(8,128)}, u32[]{:S(2)}, u32[]{:S(2)}) %all-to-all-start) | async-done | bytes 2097184 | tf_op jit(solution)/shard_map/all_to_all | solution.py:512
  44.5 4.6 %all-to-all-start.1 = ((f32[16,128,256]{2,1,0:T(8,128)}), f32[16,128,256]{2,1,0:T(8,128)}, u32[]{:S(2)}, u32[]{:S(2)}) async-start(f32[16,128,256]{2,1,0:T(8,128)} %bitcast.23), calls=%async_computation.1 | async-start | bytes 4194304 | tf_op jit(solution)/shard_map/all_to_all | solution.py:512
  49.8 5.8 %row_tree.2 = (f32[2,2,256,256]{3,2,1,0:T(8,128)}, f32[2,2,256,256]{3,2,1,0:T(8,128)}) custom-call(s32[2]{0:T(128)} %pad_add_fusion.place, f32[2048,256]{1,0:T(8,128)} %bitcast.5.x_ref, bf16[2,8,2,256,256]{4,3,2,1,0:T(8,128)(2,1)} %get-tuple-element.32.g_ref), custom_call_target="tpu_custom_call" | custom-call | flops 3000000000 | bytes 8388608 | tf_op jit(solution)/shard_map/row_tree/pallas_call | solution.py:347
  55.6 3.2 %collective-permute-start = (f32[1024,256]{1,0:T(8,128)}, f32[1024,256]{1,0:T(8,128)}, u32[]{:S(2)}, u32[]{:S(2)}) collective-permute-start(f32[1024,256]{1,0:T(8,128)} %bitcast.31), channel_id=1, source_target_pairs={{0,16},{16,0},{32,48},{48,32},{64,80},{80,64},{96,112},{112,96},{1... | collective-permute-start | bytes 3145736 | tf_op jit(solution)/shard_map/ppermute | solution.py:542
  58.8 15.7 %all-to-all-done.1 = f32[16,128,256]{2,1,0:T(8,128)} async-done(((f32[16,128,256]{2,1,0:T(8,128)}), f32[16,128,256]{2,1,0:T(8,128)}, u32[]{:S(2)}, u32[]{:S(2)}) %all-to-all-start.1) | async-done | bytes 2097184 | tf_op jit(solution)/shard_map/all_to_all | solution.py:512
  74.5 5.8 %row_tree.3 = (f32[2,2,256,256]{3,2,1,0:T(8,128)}, f32[2,2,256,256]{3,2,1,0:T(8,128)}) custom-call(s32[2]{0:T(128)} %pad_add_fusion.place, f32[2048,256]{1,0:T(8,128)} %bitcast.12.x_ref, bf16[2,8,2,256,256]{4,3,2,1,0:T(8,128)(2,1)} %get-tuple-element.32.g_ref), custom_call_target="tpu_custom_call" | custom-call | flops 3000000000 | bytes 8388608 | tf_op jit(solution)/shard_map/row_tree/pallas_call | solution.py:347
  80.3 5.5 %collective-permute-start.7 = (f32[1024,256]{1,0:T(8,128)}, f32[1024,256]{1,0:T(8,128)}, u32[]{:S(2)}, u32[]{:S(2)}) collective-permute-start(f32[1024,256]{1,0:T(8,128)} %bitcast.30), channel_id=1, source_target_pairs={{0,16},{16,0},{32,48},{48,32},{64,80},{80,64},{96,112},{112,96},{1... | collective-permute-start | bytes 3145736 | tf_op jit(solution)/shard_map/ppermute | solution.py:542
  85.8 3.0 %add_halves.2 = (f32[256,256]{1,0:T(8,128)}, f32[256,256]{1,0:T(8,128)}, f32[256,256]{1,0:T(8,128)}, f32[256,256]{1,0:T(8,128)}) custom-call(s32[2]{0:T(128)} %pad_add_fusion.place, f32[1024,256]{1,0:T(8,128)} %bitcast.27, f32[1024,256]{1,0:T(8,128)} %collective-permute-done.got_ref), custom_call_target="tpu_custom_call" | custom-call | flops 262144 | bytes 3145728 | tf_op jit(solution)/shard_map/add_halves/pallas_call | solution.py:389
  88.9 2.2 collective-permute-start.2
  91.1 5.9 %collective-permute-done.1.refs_1_ = f32[256,256]{1,0:T(8,128)} collective-permute-done((f32[256,256]{1,0:T(8,128)}, f32[256,256]{1,0:T(8,128)}, u32[]{:S(2)}, u32[]{:S(2)}) %collective-permute-start.1) | collective-permute-done | bytes 262176 | tf_op jit(solution)/shard_map/ppermute | solution.py:552
  98.5 6.1 %collective-permute-done.3.refs_3_ = f32[256,256]{1,0:T(8,128)} collective-permute-done((f32[256,256]{1,0:T(8,128)}, f32[256,256]{1,0:T(8,128)}, u32[]{:S(2)}, u32[]{:S(2)}) %collective-permute-start.3) | collective-permute-done | bytes 262176 | tf_op jit(solution)/shard_map/ppermute | solution.py:552
  104.6 2.1 add_pieces.2.refs_0_
  109.6 3.0 %add_halves.3 = (f32[256,256]{1,0:T(8,128)}, f32[256,256]{1,0:T(8,128)}, f32[256,256]{1,0:T(8,128)}, f32[256,256]{1,0:T(8,128)}) custom-call(s32[2]{0:T(128)} %pad_add_fusion.place, f32[1024,256]{1,0:T(8,128)} %bitcast.26, f32[1024,256]{1,0:T(8,128)} %collective-permute-done.7.got_ref), custom_call_target="tpu_custom_call" | custom-call | flops 262144 | bytes 3145728 | tf_op jit(solution)/shard_map/add_halves/pallas_call | solution.py:389
  112.6 2.1 collective-permute-start.18
  114.7 6.5 %collective-permute-done.6.refs_3_ = f32[256,256]{1,0:T(8,128)} collective-permute-done((f32[256,256]{1,0:T(8,128)}, f32[256,256]{1,0:T(8,128)}, u32[]{:S(2)}, u32[]{:S(2)}) %collective-permute-start.6) | collective-permute-done | bytes 262176 | tf_op jit(solution)/shard_map/ppermute | solution.py:556
  125.5 7.4 %weigh_back.2 = (f32[2048,512]{1,0:T(8,128)}, f32[2048,256]{1,0:T(8,128)}) custom-call(s32[2]{0:T(128)} %pad_add_fusion.place, f32[256,256]{1,0:T(8,128)} %add_pieces.2.refs_0_, f32[256,256]{1,0:T(8,128)} %collective-permute-done.4.refs_1_, f32[256,256]{1,0:T(8,128)} %collective-permute-done.5.refs_2_, f32[256,256]{1,0:T(8,128)} %collective-permute-done.6.refs_3_, ...), custom_call_target="tpu_custom_call" | custom-call | flops 3000000000 | bytes 12582912 | tf_op jit(solution)/shard_map/weigh_back/pallas_call | solution.py:491
  133.0 4.6 %all-to-all-start.3 = ((f32[16,128,256]{2,1,0:T(8,128)}), f32[16,128,256]{2,1,0:T(8,128)}, u32[]{:S(2)}, u32[]{:S(2)}) async-start(f32[16,128,256]{2,1,0:T(8,128)} %bitcast.22), calls=%async_computation.3 | async-start | bytes 4194304 | tf_op jit(solution)/shard_map/all_to_all | solution.py:512
  137.6 2.3 %collective-permute-start.8 = (f32[256,256]{1,0:T(8,128)S(1)}, f32[256,256]{1,0:T(8,128)}, u32[]{:S(2)}, u32[]{:S(2)}) collective-permute-start(f32[256,256]{1,0:T(8,128)S(1)} %copy-done.9), channel_id=1, source_target_pairs={{0,32},{16,48},{32,64},{48,80},{64,96},{80,112},{96,0},{112,16},{1... | collective-permute-start | bytes 786440 | tf_op jit(solution)/shard_map/ppermute | solution.py:552
  140.6 5.1 %collective-permute-done.8.refs_1_ = f32[256,256]{1,0:T(8,128)} collective-permute-done((f32[256,256]{1,0:T(8,128)S(1)}, f32[256,256]{1,0:T(8,128)}, u32[]{:S(2)}, u32[]{:S(2)}) %collective-permute-start.8) | collective-permute-done | bytes 262176 | tf_op jit(solution)/shard_map/ppermute | solution.py:552
  145.7 3.1 %collective-permute-done.9.refs_2_ = f32[256,256]{1,0:T(8,128)} collective-permute-done((f32[256,256]{1,0:T(8,128)S(1)}, f32[256,256]{1,0:T(8,128)}, u32[]{:S(2)}, u32[]{:S(2)}) %collective-permute-start.9) | collective-permute-done | bytes 262176 | tf_op jit(solution)/shard_map/ppermute | solution.py:552
  148.8 6.1 %collective-permute-done.10.refs_3_ = f32[256,256]{1,0:T(8,128)} collective-permute-done((f32[256,256]{1,0:T(8,128)S(1)}, f32[256,256]{1,0:T(8,128)}, u32[]{:S(2)}, u32[]{:S(2)}) %collective-permute-start.10) | collective-permute-done | bytes 262176 | tf_op jit(solution)/shard_map/ppermute | solution.py:552
  161.0 10.2 %collective-permute-done.13.refs_3_ = f32[256,256]{1,0:T(8,128)S(1)} collective-permute-done((f32[256,256]{1,0:T(8,128)}, f32[256,256]{1,0:T(8,128)S(1)}, u32[]{:S(2)}, u32[]{:S(2)}) %collective-permute-start.13) | collective-permute-done | bytes 262176 | tf_op jit(solution)/shard_map/ppermute | solution.py:556
  176.4 7.5 %weigh_back.3 = (f32[2048,512]{1,0:T(8,128)}, f32[2048,256]{1,0:T(8,128)}) custom-call(s32[2]{0:T(128)} %pad_add_fusion.place, f32[256,256]{1,0:T(8,128)} %add_pieces.3.refs_0_, f32[256,256]{1,0:T(8,128)} %copy-done.2, f32[256,256]{1,0:T(8,128)} %copy-done.1, f32[256,256]{1,0:T(8,128)} %copy-done, ...), custom_call_target="tpu_custom_call", output_to_operand_aliasing={{0}: (11, {})} | custom-call | flops 3000000000 | bytes 12582912 | tf_op jit(solution)/shard_map/weigh_back/pallas_call | solution.py:491
  184.0 6.6 %all-to-all-start.2 = ((f32[16,128,256]{2,1,0:T(8,128)}), f32[16,128,256]{2,1,0:T(8,128)}, u32[]{:S(2)}, u32[]{:S(2)}) async-start(f32[16,128,256]{2,1,0:T(8,128)} %bitcast.24), calls=%async_computation.2 | async-start | bytes 4194304 | tf_op jit(solution)/shard_map/all_to_all | solution.py:512
  190.6 7.4 %column_back.2.rest_0_ = f32[2048,512]{1,0:T(8,128)} custom-call(f32[2,2,512,256]{3,2,1,0:T(8,128)} %bitcast.18.x_ref, bf16[16,256,128]{2,1,0:T(8,128)(2,1)} %get-tuple-element.59.w_ref, bf16[2,8,2,256,256]{4,3,2,1,0:T(8,128)(2,1)} %get-tuple-element.60.g_ref), custom_call_target="tpu_custom_call" | custom-call | flops 4000000000 | bytes 9437184 | tf_op jit(solution)/shard_map/column_back/pallas_call | solution.py:314
  198.0 21.9 %all-to-all-done.2 = f32[16,128,256]{2,1,0:T(8,128)} async-done(((f32[16,128,256]{2,1,0:T(8,128)}), f32[16,128,256]{2,1,0:T(8,128)}, u32[]{:S(2)}, u32[]{:S(2)}) %all-to-all-start.2) | async-done | bytes 2097184 | tf_op jit(solution)/shard_map/all_to_all | solution.py:512
  219.9 7.4 %column_back.3 = f32[2048,512]{1,0:T(8,128)} custom-call(f32[2,2,512,256]{3,2,1,0:T(8,128)} %bitcast.16.x_ref, bf16[16,256,128]{2,1,0:T(8,128)(2,1)} %get-tuple-element.59.w_ref, bf16[2,8,2,256,256]{4,3,2,1,0:T(8,128)(2,1)} %get-tuple-element.60.g_ref, f32[2048,512]{1,0:T(8,128)} %column_back.2.rest_0_), custom_call_target="tpu_custom_call", output_to_operand_aliasing={{}: (3, {})} | custom-call | flops 4000000000 | bytes 9437184 | tf_op jit(solution)/shard_map/column_back/pallas_call | solution.py:314
  (55 shorter events, 21.3 us)
Async XLA Ops:
  8.7 35.9 %all-to-all-start = ((f32[16,128,256]{2,1,0:T(8,128)}), f32[16,128,256]{2,1,0:T(8,128)}, u32[]{:S(2)}, u32[]{:S(2)}) async-start(f32[16,128,256]{2,1,0:T(8,128)} %bitcast.25), calls=%async_computation | async-start | bytes 4194304 | tf_op jit(solution)/shard_map/all_to_all | solution.py:512
  44.5 29.9 %all-to-all-start.1 = ((f32[16,128,256]{2,1,0:T(8,128)}), f32[16,128,256]{2,1,0:T(8,128)}, u32[]{:S(2)}, u32[]{:S(2)}) async-start(f32[16,128,256]{2,1,0:T(8,128)} %bitcast.23), calls=%async_computation.1 | async-start | bytes 4194304 | tf_op jit(solution)/shard_map/all_to_all | solution.py:512
  55.6 30.2 %collective-permute-start = (f32[1024,256]{1,0:T(8,128)}, f32[1024,256]{1,0:T(8,128)}, u32[]{:S(2)}, u32[]{:S(2)}) collective-permute-start(f32[1024,256]{1,0:T(8,128)} %bitcast.31), channel_id=1, source_target_pairs={{0,16},{16,0},{32,48},{48,32},{64,80},{80,64},{96,112},{112,96},{1... | collective-permute-start | bytes 3145736 | tf_op jit(solution)/shard_map/ppermute | solution.py:542
  80.3 29.3 %collective-permute-start.7 = (f32[1024,256]{1,0:T(8,128)}, f32[1024,256]{1,0:T(8,128)}, u32[]{:S(2)}, u32[]{:S(2)}) collective-permute-start(f32[1024,256]{1,0:T(8,128)} %bitcast.30), channel_id=1, source_target_pairs={{0,16},{16,0},{32,48},{48,32},{64,80},{80,64},{96,112},{112,96},{1... | collective-permute-start | bytes 3145736 | tf_op jit(solution)/shard_map/ppermute | solution.py:542
  88.8 8.2 %collective-permute-start.1 = (f32[256,256]{1,0:T(8,128)}, f32[256,256]{1,0:T(8,128)}, u32[]{:S(2)}, u32[]{:S(2)}) collective-permute-start(f32[256,256]{1,0:T(8,128)} %get-tuple-element.36), channel_id=1, source_target_pairs={{0,32},{16,48},{32,64},{48,80},{64,96},{80,112},{96,0},{112,16},{1... | collective-permute-start | bytes 786440 | tf_op jit(solution)/shard_map/ppermute | solution.py:552
  88.9 9.7 %collective-permute-start.2 = (f32[256,256]{1,0:T(8,128)}, f32[256,256]{1,0:T(8,128)}, u32[]{:S(2)}, u32[]{:S(2)}) collective-permute-start(f32[256,256]{1,0:T(8,128)} %get-tuple-element.37), channel_id=1, source_target_pairs={{0,64},{16,80},{32,96},{48,112},{64,0},{80,16},{96,32},{112,48},{1... | collective-permute-start | bytes 786440 | tf_op jit(solution)/shard_map/ppermute | solution.py:552
  91.1 13.5 %collective-permute-start.3 = (f32[256,256]{1,0:T(8,128)}, f32[256,256]{1,0:T(8,128)}, u32[]{:S(2)}, u32[]{:S(2)}) collective-permute-start(f32[256,256]{1,0:T(8,128)} %get-tuple-element.38), channel_id=1, source_target_pairs={{0,96},{16,112},{32,0},{48,16},{64,32},{80,48},{96,64},{112,80},{1... | collective-permute-start | bytes 786440 | tf_op jit(solution)/shard_map/ppermute | solution.py:552
  106.7 14.6 %collective-permute-start.6 = (f32[256,256]{1,0:T(8,128)}, f32[256,256]{1,0:T(8,128)}, u32[]{:S(2)}, u32[]{:S(2)}) collective-permute-start(f32[256,256]{1,0:T(8,128)} %add_pieces.2.refs_0_), channel_id=1, source_target_pairs={{0,96},{16,112},{32,0},{48,16},{64,32},{80,48},{96,64},{112,80},{1... | collective-permute-start | bytes 786440 | tf_op jit(solution)/shard_map/ppermute | solution.py:556
  106.8 14.5 %collective-permute-start.5 = (f32[256,256]{1,0:T(8,128)}, f32[256,256]{1,0:T(8,128)}, u32[]{:S(2)}, u32[]{:S(2)}) collective-permute-start(f32[256,256]{1,0:T(8,128)} %add_pieces.2.refs_0_), channel_id=1, source_target_pairs={{0,64},{16,80},{32,96},{48,112},{64,0},{80,16},{96,32},{112,48},{1... | collective-permute-start | bytes 786440 | tf_op jit(solution)/shard_map/ppermute | solution.py:556
  108.4 13.3 %collective-permute-start.4 = (f32[256,256]{1,0:T(8,128)}, f32[256,256]{1,0:T(8,128)}, u32[]{:S(2)}, u32[]{:S(2)}) collective-permute-start(f32[256,256]{1,0:T(8,128)} %add_pieces.2.refs_0_), channel_id=1, source_target_pairs={{0,32},{16,48},{32,64},{48,80},{64,96},{80,112},{96,0},{112,16},{1... | collective-permute-start | bytes 786440 | tf_op jit(solution)/shard_map/ppermute | solution.py:556
  112.6 11.1 %collective-permute-start.18 = (f32[256,256]{1,0:T(8,128)}, f32[256,256]{1,0:T(8,128)}, u32[]{:S(2)}, u32[]{:S(2)}) collective-permute-start(f32[256,256]{1,0:T(8,128)} %add_pieces.2.refs_0_), channel_id=1, source_target_pairs={{0,16},{16,0},{32,48},{48,32},{64,80},{80,64},{96,112},{112,96},{1... | collective-permute-start | bytes 786440 | tf_op jit(solution)/shard_map/ppermute | solution.py:560
  121.7 3.1 %collective-permute-start.19 = (f32[256,256]{1,0:T(8,128)}, f32[256,256]{1,0:T(8,128)}, u32[]{:S(2)}, u32[]{:S(2)}) collective-permute-start(f32[256,256]{1,0:T(8,128)} %collective-permute-done.4.refs_1_), channel_id=1, source_target_pairs={{0,16},{16,0},{32,48},{48,32},{64,80},{80,64},{96,112},{112,96},{1... | collective-permute-start | bytes 786440 | tf_op jit(solution)/shard_map/ppermute | solution.py:560
  123.2 1.9 collective-permute-start.20
  123.2 2.3 collective-permute-start.21
  133.0 4.6 %copy-start.9 = (f32[256,256]{1,0:T(8,128)S(1)}, f32[256,256]{1,0:T(8,128)}, u32[]{:S(2)}) copy-start(f32[256,256]{1,0:T(8,128)} %get-tuple-element.49) | copy-start | bytes 786436
  133.0 6.9 %copy-start.8 = (f32[256,256]{1,0:T(8,128)S(1)}, f32[256,256]{1,0:T(8,128)}, u32[]{:S(2)}) copy-start(f32[256,256]{1,0:T(8,128)} %get-tuple-element.50) | copy-start | bytes 786436
  133.0 6.9 %copy-start.7 = (f32[256,256]{1,0:T(8,128)S(1)}, f32[256,256]{1,0:T(8,128)}, u32[]{:S(2)}) copy-start(f32[256,256]{1,0:T(8,128)} %get-tuple-element.51) | copy-start | bytes 786436
  133.0 51.0 %all-to-all-start.3 = ((f32[16,128,256]{2,1,0:T(8,128)}), f32[16,128,256]{2,1,0:T(8,128)}, u32[]{:S(2)}, u32[]{:S(2)}) async-start(f32[16,128,256]{2,1,0:T(8,128)} %bitcast.22), calls=%async_computation.3 | async-start | bytes 4194304 | tf_op jit(solution)/shard_map/all_to_all | solution.py:512
  137.6 8.1 %collective-permute-start.8 = (f32[256,256]{1,0:T(8,128)S(1)}, f32[256,256]{1,0:T(8,128)}, u32[]{:S(2)}, u32[]{:S(2)}) collective-permute-start(f32[256,256]{1,0:T(8,128)S(1)} %copy-done.9), channel_id=1, source_target_pairs={{0,32},{16,48},{32,64},{48,80},{64,96},{80,112},{96,0},{112,16},{1... | collective-permute-start | bytes 786440 | tf_op jit(solution)/shard_map/ppermute | solution.py:552
  139.9 8.9 %collective-permute-start.9 = (f32[256,256]{1,0:T(8,128)S(1)}, f32[256,256]{1,0:T(8,128)}, u32[]{:S(2)}, u32[]{:S(2)}) collective-permute-start(f32[256,256]{1,0:T(8,128)S(1)} %copy-done.8), channel_id=1, source_target_pairs={{0,64},{16,80},{32,96},{48,112},{64,0},{80,16},{96,32},{112,48},{1... | collective-permute-start | bytes 786440 | tf_op jit(solution)/shard_map/ppermute | solution.py:552
  139.9 15.0 %collective-permute-start.10 = (f32[256,256]{1,0:T(8,128)S(1)}, f32[256,256]{1,0:T(8,128)}, u32[]{:S(2)}, u32[]{:S(2)}) collective-permute-start(f32[256,256]{1,0:T(8,128)S(1)} %copy-done.7), channel_id=1, source_target_pairs={{0,96},{16,112},{32,0},{48,16},{64,32},{80,48},{96,64},{112,80},{1... | collective-permute-start | bytes 786440 | tf_op jit(solution)/shard_map/ppermute | solution.py:552
  157.0 14.3 %collective-permute-start.13 = (f32[256,256]{1,0:T(8,128)}, f32[256,256]{1,0:T(8,128)S(1)}, u32[]{:S(2)}, u32[]{:S(2)}) collective-permute-start(f32[256,256]{1,0:T(8,128)} %add_pieces.3.refs_0_), channel_id=1, source_target_pairs={{0,96},{16,112},{32,0},{48,16},{64,32},{80,48},{96,64},{112,80},{1... | collective-permute-start | bytes 786440 | tf_op jit(solution)/shard_map/ppermute | solution.py:556
  157.0 16.4 %collective-permute-start.12 = (f32[256,256]{1,0:T(8,128)}, f32[256,256]{1,0:T(8,128)S(1)}, u32[]{:S(2)}, u32[]{:S(2)}) collective-permute-start(f32[256,256]{1,0:T(8,128)} %add_pieces.3.refs_0_), channel_id=1, source_target_pairs={{0,64},{16,80},{32,96},{48,112},{64,0},{80,16},{96,32},{112,48},{1... | collective-permute-start | bytes 786440 | tf_op jit(solution)/shard_map/ppermute | solution.py:556
  158.0 15.6 %collective-permute-start.11 = (f32[256,256]{1,0:T(8,128)}, f32[256,256]{1,0:T(8,128)S(1)}, u32[]{:S(2)}, u32[]{:S(2)}) collective-permute-start(f32[256,256]{1,0:T(8,128)} %add_pieces.3.refs_0_), channel_id=1, source_target_pairs={{0,32},{16,48},{32,64},{48,80},{64,96},{80,112},{96,0},{112,16},{1... | collective-permute-start | bytes 786440 | tf_op jit(solution)/shard_map/ppermute | solution.py:556
  159.7 14.3 %collective-permute-start.14 = (f32[256,256]{1,0:T(8,128)}, f32[256,256]{1,0:T(8,128)S(1)}, u32[]{:S(2)}, u32[]{:S(2)}) collective-permute-start(f32[256,256]{1,0:T(8,128)} %add_pieces.3.refs_0_), channel_id=1, source_target_pairs={{0,16},{16,0},{32,48},{48,32},{64,80},{80,64},{96,112},{112,96},{1... | collective-permute-start | bytes 786440 | tf_op jit(solution)/shard_map/ppermute | solution.py:560
  171.9 2.7 %collective-permute-start.17 = (f32[256,256]{1,0:T(8,128)S(1)}, f32[256,256]{1,0:T(8,128)S(1)}, u32[]{:S(2)}, u32[]{:S(2)}) collective-permute-start(f32[256,256]{1,0:T(8,128)S(1)} %collective-permute-done.13.refs_3_), channel_id=1, source_target_pairs={{0,16},{16,0},{32,48},{48,32},{64,80},{80,64},{96,112},{112,96},{1... | collective-permute-start | bytes 786440 | tf_op jit(solution)/shard_map/ppermute | solution.py:560
  173.5 1.2 copy-start.1
  173.5 1.5 collective-permute-start.16
  173.6 1.5 copy-start.2
  173.6 1.8 collective-permute-start.15
  174.0 1.4 copy-start.3
  184.0 35.9 %all-to-all-start.2 = ((f32[16,128,256]{2,1,0:T(8,128)}), f32[16,128,256]{2,1,0:T(8,128)}, u32[]{:S(2)}, u32[]{:S(2)}) async-start(f32[16,128,256]{2,1,0:T(8,128)} %bitcast.24), calls=%async_computation.2 | async-start | bytes 4194304 | tf_op jit(solution)/shard_map/all_to_all | solution.py:512
  (4 other events, 2.9 us)
where the time goes:
time: 231 us; the launch traced here: 227 us
  waiting for transfers between devices  91.3 us (40%)
  Pallas kernels  82.1 us (36%)
  starting transfers between devices  50.7 us (22%)
    all_to_all x4, waiting for transfers between devices, exchange(): lax.all_to_all(x.reshape(nodes, rows // nodes, columns), 'node', split_ax...  43.2 us
    ppermute x6, waiting for transfers between devices, shards(): got.append(lax.ppermute(pieces[d], 'block', shift[d]))  27.8 us
    all_to_all x4, starting transfers between devices, exchange(): lax.all_to_all(x.reshape(nodes, rows // nodes, columns), 'node', split_ax...  23.5 us
    pallas_call x3, Pallas kernels, merged_columns(): pl.pallas_call(functools.partial(merged_column_kernel, back, 4), grid=(3...  22.4 us
    ppermute x6, waiting for transfers between devices, shards(): mine.append(lax.ppermute(total_piece, 'block', shift[d]))  17.2 us
    pallas_call x2, Pallas kernels, weigh_back(): pl.pallas_call(functools.partial(weigh_kernel, first_bit, span, ring, chu...  14.9 us
    pallas_call x2, Pallas kernels, row_tree(): pl.pallas_call(functools.partial(row_kernel, first_bit, span), grid=(2 *...  11.6 us
    ppermute x2, starting transfers between devices, start(): got = lax.ppermute(halves[n][1], 'block', sibling)  8.72 us
  transfers between devices with their start and end apart: 26, of which 18 were waited for; matrix products, arithmetic and copies ran while one was open for 0% of the time, Pallas kernels for 26%

commit v1 on v0

v1 whole, which is shorter than its diff:
```python
import functools
import jax
import jax.numpy as jnp
from jax import lax
from jax.experimental import pallas as pl
from jax.experimental.pallas import tpu as pltpu
from jax.sharding import PartitionSpec as P


CHUNKS = 2
F32 = jnp.float32
BF16 = jnp.bfloat16
PARAMS = pltpu.CompilerParams(vmem_limit_bytes=67043328)


def split(value):
    high = value.astype(jnp.bfloat16)
    low = (value - high.astype(F32)).astype(jnp.bfloat16)
    return high, low


def pair_of(j, bit):
    first = ((j >> bit) << (bit + 1)) + (j & ((1 << bit) - 1))
    return first, first + (1 << bit)


PARTS = 4


def rows_of(c, span):
    return slice(c * span, (c + 1) * span)


def take(ref, spans, span):
    return jnp.concatenate([ref[rows_of(c, span), :] for c in spans], axis=0)


def put(ref, spans, span, value):
    for n, c in enumerate(spans):
        ref[rows_of(c, span), :] = value[n * span : (n + 1) * span]


class Copies:
    def __init__(self, sems):
        self.sems, self.used = sems, 0

    def start(self, source, target):
        copy = pltpu.make_async_copy(source, target, self.sems.at[self.used])
        self.used += 1
        copy.start()
        return copy


def wait_all(copies):
    for copy in copies:
        copy.wait()


def part_rows(rows, halves):
    size = rows // PARTS // halves
    return [[pl.ds(h * (rows // halves) + p * size, size) for h in range(halves)] for p in range(PARTS)]


def pair_product(f_high, f_low, x):
    lhs = jnp.concatenate([f_high, f_low], axis=0)
    lhs = jnp.concatenate([lhs, lhs], axis=1)
    out = jnp.dot(lhs, jnp.concatenate(split(x), axis=0), preferred_element_type=F32)
    half = out.shape[0] // 2
    return out[:half] + out[half:]


def column_kernel(chunk, ranks, x_ref, f_ref, o_ref, x_buf, f_buf, buf_a, buf_b, o_buf, sems):
    levels, count, span = f_buf.shape[:3]
    rows, columns = x_buf.shape
    copies = Copies(sems)
    at = pl.ds(chunk * columns, columns)
    first = []
    size = count // PARTS
    for p in range(PARTS):
        first.append(
            [
                copies.start(f_ref.at[0, 0, pl.ds(p * size, size)], f_buf.at[0, pl.ds(p * size, size)]),
                copies.start(x_ref.at[pl.ds(p * size * span, size * span), at], x_buf.at[pl.ds(p * size * span, size * span)]),
            ]
        )
    later = [copies.start(f_ref.at[0, level], f_buf.at[level]) for level in range(1, levels)]
    bufs = [x_buf] + [(buf_a, buf_b)[level % 2] for level in range(levels - 1)] + [o_buf]
    row_ids = lax.broadcasted_iota(jnp.int32, (span, 2 * span), 0)
    outs = []
    for level in range(levels):
        if level:
            later[level - 1].wait()
        for p in range(PARTS):
            if level == 0:
                wait_all(first[p])
            for j in range(p * size // 2, (p + 1) * size // 2):
                pair = pair_of(j, level)
                factor = jnp.concatenate(
                    [jnp.where(row_ids < ranks[level, 0, c], f_buf[level, c], 0.0) for c in pair], axis=0
                )
                put(bufs[level + 1], pair, span, pair_product(*split(factor), take(bufs[level], pair, span)))
            if level == levels - 1:
                outs += [copies.start(o_buf.at[at], o_ref.at[at]) for at in part_rows(rows, 2)[p]]
    wait_all(outs)


def column_tree(x, factors, ranks, columns, chunk):
    rows = x.shape[0]
    return pl.pallas_call(
        functools.partial(column_kernel, chunk),
        out_shape=jax.ShapeDtypeStruct((rows, columns), F32),
        in_specs=[SMEM0, HBM, HBM],
        out_specs=HBM,
        scratch_shapes=[pltpu.VMEM((rows, columns), F32), pltpu.VMEM(factors.shape[1:], F32)]
        + [pltpu.VMEM((rows, columns), F32)] * 3
        + [pltpu.SemaphoreType.DMA((32,))],
        compiler_params=PARAMS,
        cost_estimate=pl.CostEstimate(flops=5 * 10**9, transcendentals=0, bytes_accessed=9 << 20),
        name="column_tree",
    )(ranks, x, factors)


SMEM0 = pl.BlockSpec(memory_space=pltpu.SMEM)
HBM = pl.BlockSpec(memory_space=pltpu.HBM)
SMEM = SMEM0


def quad_of(j, bit):
    base = ((j >> bit) << (bit + 2)) + (j & ((1 << bit) - 1))
    return [base + (n << bit) for n in range(4)]


def three(high, low, axis):
    return jnp.concatenate([high, high, low] if axis == 1 else [high, low, high], axis=axis)


def merge_kernel(first_bit, ranks, fa_ref, fb_ref, *refs):
    g_ref, t_ref = refs[-2:]
    span = fa_ref.shape[-2]
    lane = lax.broadcasted_iota(jnp.int32, (2 * span, 2 * span), 1)
    row_ids = lax.broadcasted_iota(jnp.int32, (span, 2 * span), 0)
    for s in range(2):

        @pl.when(pl.program_id(0) == s)
        def _(s=s):
            bit = first_bit + 2 * s
            masked = lambda ref, level, c: jnp.where(row_ids < ranks[level, 0, c], ref[0, c], 0.0)

            def body(j, carry):
                quad = quad_of(j, bit)
                rows = [None] * 4
                for a in range(2):
                    spans = (quad[a], quad[2 + a])
                    inner = jnp.concatenate([masked(fa_ref, 2 * s, c) for c in spans], axis=0)
                    outer = jnp.concatenate([masked(fb_ref, 2 * s + 1, c) for c in spans], axis=0)
                    outer = jnp.concatenate([jnp.where(lane < span, outer, 0.0), jnp.where(lane < span, 0.0, outer)], axis=0)
                    both = jnp.dot(three(*split(outer), 1), three(*split(inner), 0), preferred_element_type=F32)
                    both = jnp.concatenate([both[: 2 * span], both[2 * span :]], axis=1)
                    rows[a], rows[2 + a] = both[:span], both[span:]
                merged = jnp.concatenate(rows, axis=0)
                for out, value in ((g_ref, merged), (t_ref, merged.T)):
                    high, low = split(value)
                    out[0, j, 0] = high
                    out[0, j, 1] = low
                return carry

            lax.fori_loop(0, g_ref.shape[1], body, 0, unroll=4)


def merge_columns_kernel(first_bit, last, ranks, fa_ref, fb_ref, fe_ref, w_ref, v_ref, g_ref, t_ref):
    span = fa_ref.shape[-2]
    row_ids = lax.broadcasted_iota(jnp.int32, (span, 2 * span), 0)

    @pl.when(pl.program_id(0) == 0)
    def _():
        for j in range(w_ref.shape[0]):
            pair = pair_of(j, last)
            factor = jnp.concatenate([jnp.where(row_ids < ranks[last, 0, c], fe_ref[0, c], 0.0) for c in pair], axis=0)
            w_ref[j] = jnp.concatenate(split(factor), axis=0)
            v_ref[j] = jnp.concatenate(split(factor.T), axis=0)

    merge_kernel(first_bit, ranks, fa_ref, fb_ref, g_ref, t_ref)


def merge_rows_kernel(first_bit, ranks, fa_ref, fb_ref, weight_ref, b_ref, g_ref, t_ref):
    @pl.when(pl.program_id(0) == 0)
    def _():
        size = weight_ref.shape[1]
        for n in range(weight_ref.shape[0]):
            b_ref[n * size : (n + 1) * size, :] = jnp.broadcast_to(weight_ref[n : n + 1, :], (size, size)).T

    merge_kernel(first_bit, ranks, fa_ref, fb_ref, g_ref, t_ref)


def level_spec(factors, index):
    return pl.BlockSpec((None, 1) + factors.shape[2:], lambda s: (0, index(s), 0, 0, 0))


def merged_shapes(factors):
    quads, side = factors.shape[2] // 4, 4 * factors.shape[3]
    shape = jax.ShapeDtypeStruct((2, quads, 2, side, side), BF16)
    return shape, pl.BlockSpec((1, quads, 2, side, side), lambda s: (s, 0, 0, 0, 0))


def merge_columns(factors, ranks):
    shape, spec = merged_shapes(factors)
    last = factors.shape[1] - 1
    pairs, width = factors.shape[2] // 2, 2 * factors.shape[3]
    single = jax.ShapeDtypeStruct((pairs, 2 * width, width), BF16)
    single_spec = pl.BlockSpec(single.shape, lambda s: (0, 0, 0))
    return pl.pallas_call(
        functools.partial(merge_columns_kernel, 0, last),
        grid=(2,),
        out_shape=(single, single, shape, shape),
        in_specs=[SMEM]
        + [level_spec(factors, f) for f in (lambda s: 2 * s, lambda s: 2 * s + 1, lambda s: last)],
        out_specs=(single_spec, single_spec, spec, spec),
        compiler_params=PARAMS,
        cost_estimate=pl.CostEstimate(flops=10**10, transcendentals=0, bytes_accessed=15 << 20),
        name="merge_columns",
    )(ranks, factors, factors, factors)


def merge_rows(factors, ranks, weights, first_bit):
    shape, spec = merged_shapes(factors)
    weights = weights.reshape(-1, 128)
    rows = weights.size
    return pl.pallas_call(
        functools.partial(merge_rows_kernel, first_bit),
        grid=(2,),
        out_shape=(jax.ShapeDtypeStruct((rows, 128), F32), shape, shape),
        in_specs=[SMEM] + [level_spec(factors, f) for f in (lambda s: 2 * s, lambda s: 2 * s + 1)] + [whole2(weights.shape)],
        out_specs=(whole2((rows, 128)), spec, spec),
        compiler_params=PARAMS,
        cost_estimate=pl.CostEstimate(flops=10**10, transcendentals=0, bytes_accessed=12 << 20),
        name="merge_rows",
    )(ranks, factors, factors, weights)


def whole2(shape):
    return pl.BlockSpec(shape, lambda s: (0, 0))


def quad_product(g_ref, x):
    return jnp.dot(three(g_ref[0], g_ref[1], 1), three(*split(x), 0), preferred_element_type=F32)


def start_merged(copies, g_ref, g_buf, stage):
    size = g_buf.shape[1] // PARTS
    return [copies.start(g_ref.at[stage, pl.ds(p * size, size)], g_buf.at[stage, pl.ds(p * size, size)]) for p in range(PARTS)]


def quad_stage(g_buf, stage, bit, load, store, ready, done=None):
    size = g_buf.shape[1] // PARTS
    for p in range(PARTS):
        ready(p)
        for j in range(p * size, (p + 1) * size):
            quad = quad_of(j, bit)
            store(quad, quad_product(g_buf.at[stage, j], load(quad)))
        if done:
            done(p)


def merged_column_kernel(back, chunk, x_ref, w_ref, g_ref, *rest):
    o_ref, x_buf, w_buf, g_buf, buf_a, buf_b, o_buf, sems = rest[-8:]
    span = w_buf.shape[-1] // 2
    rows, columns = x_buf.shape
    at = pl.ds(chunk * columns, columns)
    copies = Copies(sems)
    w_size = w_buf.shape[0] // PARTS
    start_single = lambda p: copies.start(w_ref.at[pl.ds(p * w_size, w_size)], w_buf.at[pl.ds(p * w_size, w_size)])
    run_in, run_out = part_rows(rows, 2 if back else 1), part_rows(rows, 1 if back else 2)
    get = lambda p: [copies.start(x_ref.at[r] if back else x_ref.at[r, at], x_buf.at[r]) for r in run_in[p]]
    outs = []

    def leave(p):
        for r in run_out[p]:
            outs.append(copies.start(o_buf.at[r], o_ref.at[r, at] if back else o_ref.at[r]))

    def pairs(source, target, ready, done):
        for p in range(PARTS):
            ready(p)
            for j in range(p * w_size, (p + 1) * w_size):
                pair = pair_of(j, 4)
                high, low = w_buf[j, : 2 * span], w_buf[j, 2 * span :]
                put(target, pair, span, pair_product(high, low, take(source, pair, span)))
            done(p)

    def quads(stage, bit, source, target, ready, done=None):
        quad_stage(
            g_buf, stage, bit,
            lambda quad: take(source, quad, span), lambda quad, value: put(target, quad, span, value), ready, done,
        )

    if back:
        entry = [get(p) + [start_single(p)] for p in range(PARTS)]
        g_copies = {stage: start_merged(copies, g_ref, g_buf, stage) for stage in (1, 0)}
        pairs(x_buf, buf_a, lambda p: wait_all(entry[p]), lambda p: None)
        quads(1, 2, buf_a, buf_b, lambda p: g_copies[1][p].wait())
        quads(0, 0, buf_b, o_buf, lambda p: g_copies[0][p].wait(), leave)
    else:
        size = g_buf.shape[1] // PARTS
        entry = []
        for p in range(PARTS):
            g_part = copies.start(g_ref.at[0, pl.ds(p * size, size)], g_buf.at[0, pl.ds(p * size, size)])
            entry.append(get(p) + [g_part])
        g_copies = start_merged(copies, g_ref, g_buf, 1)
        singles = [start_single(p) for p in range(PARTS)]
        quads(0, 0, x_buf, buf_a, lambda p: wait_all(entry[p]))
        quads(1, 2, buf_a, buf_b, lambda p: g_copies[p].wait())
        pairs(buf_b, o_buf, lambda p: singles[p].wait(), leave)
    wait_all(outs)


def merged_columns(x, single, merged, back, columns, chunk=0, into=None, total=None, after=()):
    rows = x.shape[0]
    extra = list(after) if into is None else [into] + list(after)
    return pl.pallas_call(
        functools.partial(merged_column_kernel, back, chunk),
        out_shape=jax.ShapeDtypeStruct((rows, total or columns), F32),
        in_specs=[HBM] * 3 + [pl.BlockSpec(memory_space=pl.ANY)] * len(extra),
        out_specs=HBM,
        scratch_shapes=[pltpu.VMEM((rows, columns), F32), pltpu.VMEM(single.shape, BF16), pltpu.VMEM(merged.shape, BF16)]
        + [pltpu.VMEM((rows, columns), F32)] * 3
        + [pltpu.SemaphoreType.DMA((32,))],
        input_output_aliases={} if into is None else {3: 0},
        compiler_params=PARAMS,
        cost_estimate=pl.CostEstimate(flops=4 * 10**9, transcendentals=0, bytes_accessed=9 << 20),
        name="column_back" if back else "column_tree_merged",
    )(x, single, merged, *extra)


def row_kernel(first_bit, span, place, x_ref, g_ref, keep_ref, send_ref, x_buf, g_buf, buf, keep_buf, send_buf, sems):
    swap = place[1] == 1
    rows = x_buf.shape[0]
    copies = Copies(sems)
    size = g_buf.shape[1] // PARTS
    entry, outs = [], []
    for p in range(PARTS):
        r = part_rows(rows, 1)[p][0]
        g_part = copies.start(g_ref.at[0, pl.ds(p * size, size)], g_buf.at[0, pl.ds(p * size, size)])
        entry.append([g_part, copies.start(x_ref.at[r], x_buf.at[r])])
    g_copies = start_merged(copies, g_ref, g_buf, 1)

    def store(quad, value):
        half = 2 * span
        low, high = value[:half], value[half:]
        put(keep_buf, quad[:2], span, jnp.where(swap, high, low))
        put(send_buf, quad[:2], span, jnp.where(swap, low, high))

    def leave(p):
        for r in part_rows(rows // 2, 2)[p]:
            outs.append(copies.start(send_buf.at[r], send_ref.at[r]))
            outs.append(copies.start(keep_buf.at[r], keep_ref.at[r]))

    load = lambda ref: lambda quad: take(ref, quad, span)
    quad_stage(
        g_buf, 0, first_bit, load(x_buf), lambda quad, value: put(buf, quad, span, value), lambda p: wait_all(entry[p])
    )
    quad_stage(g_buf, 1, first_bit + 2, load(buf), store, lambda p: g_copies[p].wait(), leave)
    wait_all(outs)


def row_tree(x, merged, place, first_bit, span):
    rows, columns = x.shape
    half = jax.ShapeDtypeStruct((rows // 2, columns), F32)
    return pl.pallas_call(
        functools.partial(row_kernel, first_bit, span),
        out_shape=(half, half),
        in_specs=[SMEM0, HBM, HBM],
        out_specs=(HBM, HBM),
        scratch_shapes=[pltpu.VMEM((rows, columns), F32), pltpu.VMEM(merged.shape, BF16), pltpu.VMEM((rows, columns), F32)]
        + [pltpu.VMEM(half.shape, F32)] * 2
        + [pltpu.SemaphoreType.DMA((32,))],
        compiler_params=PARAMS,
        cost_estimate=pl.CostEstimate(flops=3 * 10**9, transcendentals=0, bytes_accessed=8 << 20),
        name="row_tree",
    )(place, x, merged)


def add_halves_kernel(ring, place, keep_ref, got_ref, *refs):
    outs, (k_buf, g_buf, in_sems, out_sems) = refs[:ring], refs[ring:]
    size = outs[0].shape[0]
    copies = []
    for d in range(ring):
        rows = pl.ds(pl.multiple_of(lax.rem(place[0] + d, ring) * size, size), size)
        copies.append(pltpu.make_async_copy(keep_ref.at[rows], k_buf.at[d], in_sems.at[0, d]))
        copies.append(pltpu.make_async_copy(got_ref.at[rows], g_buf.at[d], in_sems.at[1, d]))
    for copy in copies:
        copy.start()
    sends = []
    for d, out in enumerate(outs):
        copies[2 * d].wait()
        copies[2 * d + 1].wait()
        g_buf[d] = g_buf[d] + k_buf[d]
        sends.append(pltpu.make_async_copy(g_buf.at[d], out, out_sems.at[d]))
        sends[-1].start()
    for send in sends:
        send.wait()


def add_halves(keep, got, place, ring):
    rows, columns = keep.shape
    size = rows // ring
    piece = jax.ShapeDtypeStruct((size, columns), F32)
    return pl.pallas_call(
        functools.partial(add_halves_kernel, ring),
        out_shape=(piece,) * ring,
        in_specs=[SMEM0, HBM, HBM],
        out_specs=(HBM,) * ring,
        scratch_shapes=[pltpu.VMEM((ring, size, columns), F32)] * 2
        + [pltpu.SemaphoreType.DMA((2, ring)), pltpu.SemaphoreType.DMA((ring,))],
        compiler_params=PARAMS,
        cost_estimate=pl.CostEstimate(flops=keep.size, transcendentals=0, bytes_accessed=12 * keep.size),
        name="add_halves",
    )(place, keep, got)


def add_pieces_kernel(count, *refs):
    pieces, out = refs[:count], refs[count]
    buf, in_sems, out_sems = refs[count + 1 :]
    parts = buf.shape[1]
    size = out.shape[0] // parts
    copies = []
    for p in range(parts):
        for n, piece in enumerate(pieces):
            copies.append(pltpu.make_async_copy(piece.at[pl.ds(p * size, size)], buf.at[n, p], in_sems.at[n, p]))
            copies[-1].start()
    sends = []
    for p in range(parts):
        for n in range(count):
            copies[p * count + n].wait()
        total = buf[0, p]
        for n in range(1, count):
            total = total + buf[n, p]
        buf[0, p] = total
        sends.append(pltpu.make_async_copy(buf.at[0, p], out.at[pl.ds(p * size, size)], out_sems.at[p]))
        sends[-1].start()
    for send in sends:
        send.wait()


def add_pieces(pieces):
    rows, columns = pieces[0].shape
    count, parts = len(pieces), 2
    return pl.pallas_call(
        functools.partial(add_pieces_kernel, count),
        out_shape=jax.ShapeDtypeStruct((rows, columns), F32),
        in_specs=[HBM] * count,
        out_specs=HBM,
        scratch_shapes=[pltpu.VMEM((count, parts, rows // parts, columns), F32)]
        + [pltpu.SemaphoreType.DMA((count, parts)), pltpu.SemaphoreType.DMA((parts,))],
        compiler_params=PARAMS,
        cost_estimate=pl.CostEstimate(flops=4 * pieces[0].size, transcendentals=0, bytes_accessed=20 * pieces[0].size),
        name="add_pieces",
    )(*pieces)


def weigh_kernel(first_bit, span, ring, chunk, place, *refs):
    pieces = refs[: 2 * ring]
    w_ref, g_ref = refs[2 * ring : 2 * ring + 2]
    b_ref, o_ref, x_buf, w_buf, g_buf, buf, o_buf, sems = refs[-8:]
    size, columns = pieces[0].shape
    rows = x_buf.shape[0]
    copies = Copies(sems)
    entry, outs = [], []
    for n, piece in enumerate(pieces):
        side, d = divmod(n, ring)
        half = place[1] if side == 0 else 1 - place[1]
        begin = half * (ring * size) + lax.rem(place[0] + ring - d, ring) * size
        entry.append(copies.start(piece, x_buf.at[pl.ds(pl.multiple_of(begin, size), size)]))
    entry.append(copies.start(w_ref, w_buf))
    g_copies = {stage: start_merged(copies, g_ref, g_buf, stage) for stage in (1, 0)}
    wait_all(entry)
    block_out = copies.start(x_buf, b_ref.at[:, pl.ds(chunk * columns, columns)])

    def weighted(quad):
        value, weight = take(x_buf, quad, span), take(w_buf, quad, span)
        return value * jnp.concatenate([weight] * (columns // weight.shape[1]), axis=1)

    def leave(p):
        r = part_rows(rows, 1)[p][0]
        outs.append(copies.start(o_buf.at[r], o_ref.at[r]))

    quad_stage(
        g_buf, 1, first_bit + 2, weighted, lambda quad, value: put(buf, quad, span, value), lambda p: g_copies[1][p].wait()
    )
    quad_stage(
        g_buf, 0, first_bit, lambda quad: take(buf, quad, span),
        lambda quad, value: put(o_buf, quad, span, value), lambda p: g_copies[0][p].wait(), leave,
    )
    wait_all(outs + [block_out])


def weigh_back(pieces, weights, merged, place, first_bit, span, into, chunk, total):
    ring = len(pieces) // 2
    size, columns = pieces[0].shape
    rows = 2 * ring * size
    extra = [] if into is None else [into]
    return pl.pallas_call(
        functools.partial(weigh_kernel, first_bit, span, ring, chunk),
        out_shape=(jax.ShapeDtypeStruct((rows, total), F32), jax.ShapeDtypeStruct((rows, columns), F32)),
        in_specs=[SMEM0] + [HBM] * (len(pieces) + 2 + len(extra)),
        out_specs=(HBM, HBM),
        scratch_shapes=[pltpu.VMEM((rows, columns), F32), pltpu.VMEM(weights.shape, F32), pltpu.VMEM(merged.shape, BF16)]
        + [pltpu.VMEM((rows, columns), F32)] * 2
        + [pltpu.SemaphoreType.DMA((32,))],
        input_output_aliases={3 + len(pieces): 0} if extra else {},
        compiler_params=PARAMS,
        cost_estimate=pl.CostEstimate(flops=3 * 10**9, transcendentals=0, bytes_accessed=12 << 20),
        name="weigh_back",
    )(place, *pieces, weights, merged, *extra)


def exchange(x):
    nodes = lax.axis_size("node")
    rows, columns = x.shape
    out = lax.all_to_all(x.reshape(nodes, rows // nodes, columns), "node", split_axis=0, concat_axis=0, tiled=True)
    return out.reshape(rows, columns)


def shards(vectors, col_factors, row_factors, col_ranks, row_ranks, row_weights):
    rows, total = vectors.shape[1:]
    columns = total // CHUNKS
    low_bits = col_factors.shape[1] - row_factors.shape[1]
    ring = lax.axis_size("block") // 2
    sibling = [(b, b ^ 1) for b in range(2 * ring)]
    shift = [[(b, (b + 2 * d) % (2 * ring)) for b in range(2 * ring)] for d in range(ring)]
    index = lax.axis_index("block")
    place = jnp.stack([index // 2, index % 2]).astype(jnp.int32)
    span = col_factors.shape[3]
    flat = vectors.reshape(rows, total)
    col_ranks = jnp.transpose(col_ranks, (1, 0, 2))
    row_ranks = jnp.transpose(row_ranks, (1, 0, 2))
    chunks = range(CHUNKS)
    t = column_tree(flat, col_factors, col_ranks, columns, 0)
    sent = [exchange(t)]
    single, single_back, col_merged, col_back = merge_columns(col_factors, col_ranks)
    weights, row_merged, row_back = merge_rows(row_factors, row_ranks, row_weights, low_bits)
    for n in chunks[1:]:
        t = merged_columns(flat, single, col_merged, False, columns, n, after=[weights])
        sent.append(exchange(t))
    halves = []
    for n in chunks:
        halves.append(row_tree(sent[n], row_merged, place, low_bits, span))

    def start(n):
        got = lax.ppermute(halves[n][1], "block", sibling)
        return add_halves(halves[n][0], got, place, ring)

    block_row = result = None
    back = []
    pieces = start(0)
    for n in chunks:
        later = n + 1 < CHUNKS
        got = [pieces[0]]
        for d in range(1, ring):
            got.append(lax.ppermute(pieces[d], "block", shift[d]))
        total_piece = add_pieces(got)
        mine = [total_piece]
        for d in range(1, ring):
            mine.append(lax.ppermute(total_piece, "block", shift[d]))
        if later:
            pieces = start(n + 1)
            mine[1:], pieces = lax.optimization_barrier((mine[1:], pieces))
        theirs = [lax.ppermute(piece, "block", sibling) for piece in mine]
        block_row, t = weigh_back(mine + theirs, weights, row_back, place, low_bits, span, block_row, n, total)
        back.append(exchange(t))
    for n in chunks:
        result = merged_columns(back[n], single_back, col_back, True, columns, n, result, total)
    return block_row, result.reshape(1, rows, total)


def solution(mesh):
    in_specs = (
        P("block", "node", None),
        P("block", None, "node", None, None),
        P("block", None, "node", None, None),
        P("block", None, "node"),
        P("block", None, "node"),
        P("node"),
    )
    out_specs = (P("node", None), P("block", "node", None))
    return jax.shard_map(shards, mesh=mesh, in_specs=in_specs, out_specs=out_specs, check_vma=False)
```

time: 231 us -> 228 us (0.987)
  Pallas kernels: 82.1 us -> 78 us
    pallas_call x6, Pallas kernels: 42 us -> 38.7 us  [the longest x3 19.5 us: merged_columns(): pl.pallas_call(functools.partial(merged_column_kernel, back, chunk), out_...]
where the time goes in v1:
time: 228 us; the launch traced here: 225 us
  waiting for transfers between devices  92.6 us (41%)
  Pallas kernels  78 us (34%)
  starting transfers between devices  50.8 us (22%)
    all_to_all x4, waiting for transfers between devices, exchange(): lax.all_to_all(x.reshape(nodes, rows // nodes, columns), 'node', split_ax...  44.5 us
    ppermute x6, waiting for transfers between devices, shards(): got.append(lax.ppermute(pieces[d], 'block', shift[d]))  27.8 us
    all_to_all x4, starting transfers between devices, exchange(): lax.all_to_all(x.reshape(nodes, rows // nodes, columns), 'node', split_ax...  23.5 us
    pallas_call x3, Pallas kernels, merged_columns(): pl.pallas_call(functools.partial(merged_column_kernel, back, chunk), out_...  19.5 us
    ppermute x6, waiting for transfers between devices, shards(): mine.append(lax.ppermute(total_piece, 'block', shift[d]))  17.2 us
    pallas_call x2, Pallas kernels, weigh_back(): pl.pallas_call(functools.partial(weigh_kernel, first_bit, span, ring, chu...  13.7 us
    pallas_call x2, Pallas kernels, row_tree(): pl.pallas_call(functools.partial(row_kernel, first_bit, span), out_shape=...  12 us
    ppermute x2, starting transfers between devices, start(): got = lax.ppermute(halves[n][1], 'block', sibling)  8.86 us
  transfers between devices with their start and end apart: 26, of which 18 were waited for; matrix products, arithmetic and copies ran while one was open for 0% of the time, Pallas kernels for 26%

profile of v1, /device:TPU:25, one launch (start us, length us, event | category | flops | bytes accessed | tf_op | source)
XLA Modules:
  0.0 224.8 jit_solution(7028795236699781768)
XLA Ops:
  0.6 7.2 %column_tree.1 = f32[2048,256]{1,0:T(8,128)} custom-call(s32[5,1,32]{2,1,0:T(1,128)} %bitcast.25, f32[2048,512]{1,0:T(8,128)} %bitcast.22, f32[1,5,32,64,128]{4,3,2,1,0:T(8,128)} %fe_ref.1), custom_call_target="tpu_custom_call" | custom-call | flops 5000000000 | bytes 9437184 | tf_op jit(solution)/shard_map/column_tree/pallas_call | solution.py:109
  7.9 7.7 %all-to-all-start = ((f32[16,128,256]{2,1,0:T(8,128)}), f32[16,128,256]{2,1,0:T(8,128)}, u32[]{:S(2)}, u32[]{:S(2)}) async-start(f32[16,128,256]{2,1,0:T(8,128)} %bitcast.21), calls=%async_computation | async-start | bytes 4194304 | tf_op jit(solution)/shard_map/all_to_all | solution.py:518
  15.5 8.0 %merge_columns.1 = (bf16[16,256,128]{2,1,0:T(8,128)(2,1)}, bf16[16,256,128]{2,1,0:T(8,128)(2,1)}, bf16[2,8,2,256,256]{4,3,2,1,0:T(8,128)(2,1)}, bf16[2,8,2,256,256]{4,3,2,1,0:T(8,128)(2,1)}) custom-call(s32[5,1,32]{2,1,0:T(1,128)} %bitcast.26, f32[1,5,32,64,128]{4,3,2,1,0:T(8,128)} %fe_ref.1, f32[1,5,32,64,128]{4,3,2,1,0:T(8,128)} %fe_ref.1, ...), custom_call_target="tpu_custom_call" | custom-call | flops 10000000000 | bytes 15728640 | tf_op jit(solution)/shard_map/merge_columns/pallas_call | solution.py:211
  23.6 7.4 %merge_rows.1 = (f32[2048,128]{1,0:T(8,128)}, bf16[2,8,2,256,256]{4,3,2,1,0:T(8,128)(2,1)}, bf16[2,8,2,256,256]{4,3,2,1,0:T(8,128)(2,1)}) custom-call(s32[4,1,32]{2,1,0:T(1,128)} %bitcast.27, f32[1,4,32,64,128]{4,3,2,1,0:T(8,128)} %fb_ref.2, f32[1,4,32,64,128]{4,3,2,1,0:T(8,128)} %fb_ref.2, f32[16,128]{1,0:T(8,128)} %bitcast.24), custom_call_target="tpu_custom_call" | custom-call | flops 10000000000 | bytes 12582912 | tf_op jit(solution)/shard_map/merge_rows/pallas_call | solution.py:228
  30.9 6.6 %column_tree_merged.1 = f32[2048,256]{1,0:T(8,128)} custom-call(f32[2048,512]{1,0:T(8,128)} %bitcast.23, bf16[16,256,128]{2,1,0:T(8,128)(2,1)} %get-tuple-element.39.w_ref, bf16[2,8,2,256,256]{4,3,2,1,0:T(8,128)(2,1)} %get-tuple-element.40.g_ref, f32[2048,128]{1,0:T(8,128)} %get-tuple-element.41.rest_0_.refs_8_), custom_call_target="tpu_custom_call" | custom-call | flops 4000000000 | bytes 9437184 | tf_op jit(solution)/shard_map/column_tree_merged/pallas_call | solution.py:318
  37.5 6.2 %all-to-all-done = f32[16,128,256]{2,1,0:T(8,128)} async-done(((f32[16,128,256]{2,1,0:T(8,128)}), f32[16,128,256]{2,1,0:T(8,128)}, u32[]{:S(2)}, u32[]{:S(2)}) %all-to-all-start) | async-done | bytes 2097184 | tf_op jit(solution)/shard_map/all_to_all | solution.py:518
  43.8 4.6 %all-to-all-start.1 = ((f32[16,128,256]{2,1,0:T(8,128)}), f32[16,128,256]{2,1,0:T(8,128)}, u32[]{:S(2)}, u32[]{:S(2)}) async-start(f32[16,128,256]{2,1,0:T(8,128)} %bitcast.19), calls=%async_computation.1 | async-start | bytes 4194304 | tf_op jit(solution)/shard_map/all_to_all | solution.py:518
  49.0 6.0 %row_tree.2 = (f32[1024,256]{1,0:T(8,128)}, f32[1024,256]{1,0:T(8,128)}) custom-call(s32[2]{0:T(128)} %pad_add_fusion.place, f32[2048,256]{1,0:T(8,128)} %bitcast.5.x_ref, bf16[2,8,2,256,256]{4,3,2,1,0:T(8,128)(2,1)} %get-tuple-element.32.g_ref), custom_call_target="tpu_custom_call" | custom-call | flops 3000000000 | bytes 8388608 | tf_op jit(solution)/shard_map/row_tree/pallas_call | solution.py:367
  55.0 3.3 %collective-permute-start = (f32[1024,256]{1,0:T(8,128)}, f32[1024,256]{1,0:T(8,128)}, u32[]{:S(2)}, u32[]{:S(2)}) collective-permute-start(f32[1024,256]{1,0:T(8,128)} %get-tuple-element.34), channel_id=1, source_target_pairs={{0,16},{16,0},{32,48},{48,32},{64,80},{80,64},{96,112},{112,96},{1... | collective-permute-start | bytes 3145736 | tf_op jit(solution)/shard_map/ppermute | solution.py:548
  58.3 15.4 %all-to-all-done.1 = f32[16,128,256]{2,1,0:T(8,128)} async-done(((f32[16,128,256]{2,1,0:T(8,128)}), f32[16,128,256]{2,1,0:T(8,128)}, u32[]{:S(2)}, u32[]{:S(2)}) %all-to-all-start.1) | async-done | bytes 2097184 | tf_op jit(solution)/shard_map/all_to_all | solution.py:518
  73.7 6.0 %row_tree.3 = (f32[1024,256]{1,0:T(8,128)}, f32[1024,256]{1,0:T(8,128)}) custom-call(s32[2]{0:T(128)} %pad_add_fusion.place, f32[2048,256]{1,0:T(8,128)} %bitcast.10.x_ref, bf16[2,8,2,256,256]{4,3,2,1,0:T(8,128)(2,1)} %get-tuple-element.32.g_ref), custom_call_target="tpu_custom_call" | custom-call | flops 3000000000 | bytes 8388608 | tf_op jit(solution)/shard_map/row_tree/pallas_call | solution.py:367
  79.7 5.6 %collective-permute-start.7 = (f32[1024,256]{1,0:T(8,128)}, f32[1024,256]{1,0:T(8,128)}, u32[]{:S(2)}, u32[]{:S(2)}) collective-permute-start(f32[1024,256]{1,0:T(8,128)} %get-tuple-element.43), channel_id=1, source_target_pairs={{0,16},{16,0},{32,48},{48,32},{64,80},{80,64},{96,112},{112,96},{1... | collective-permute-start | bytes 3145736 | tf_op jit(solution)/shard_map/ppermute | solution.py:548
  85.3 3.0 %add_halves.2 = (f32[256,256]{1,0:T(8,128)}, f32[256,256]{1,0:T(8,128)}, f32[256,256]{1,0:T(8,128)}, f32[256,256]{1,0:T(8,128)}) custom-call(s32[2]{0:T(128)} %pad_add_fusion.place, f32[1024,256]{1,0:T(8,128)} %get-tuple-element.33.keep_ref, f32[1024,256]{1,0:T(8,128)} %collective-permute-done.got_ref), custom_call_target="tpu_custom_call" | custom-call | flops 262144 | bytes 3145728 | tf_op jit(solution)/shard_map/add_halves/pallas_call | solution.py:406
  88.4 2.2 collective-permute-start.2
  90.6 5.9 %collective-permute-done.1.refs_1_ = f32[256,256]{1,0:T(8,128)} collective-permute-done((f32[256,256]{1,0:T(8,128)}, f32[256,256]{1,0:T(8,128)}, u32[]{:S(2)}, u32[]{:S(2)}) %collective-permute-start.1) | collective-permute-done | bytes 262176 | tf_op jit(solution)/shard_map/ppermute | solution.py:558
  98.0 6.1 %collective-permute-done.3.refs_3_ = f32[256,256]{1,0:T(8,128)} collective-permute-done((f32[256,256]{1,0:T(8,128)}, f32[256,256]{1,0:T(8,128)}, u32[]{:S(2)}, u32[]{:S(2)}) %collective-permute-start.3) | collective-permute-done | bytes 262176 | tf_op jit(solution)/shard_map/ppermute | solution.py:558
  104.1 2.1 add_pieces.2.refs_0_
  109.1 3.0 %add_halves.3 = (f32[256,256]{1,0:T(8,128)}, f32[256,256]{1,0:T(8,128)}, f32[256,256]{1,0:T(8,128)}, f32[256,256]{1,0:T(8,128)}) custom-call(s32[2]{0:T(128)} %pad_add_fusion.place, f32[1024,256]{1,0:T(8,128)} %get-tuple-element.42.keep_ref, f32[1024,256]{1,0:T(8,128)} %collective-permute-done.7.got_ref), custom_call_target="tpu_custom_call" | custom-call | flops 262144 | bytes 3145728 | tf_op jit(solution)/shard_map/add_halves/pallas_call | solution.py:406
  112.1 2.1 collective-permute-start.18
  114.2 6.5 %collective-permute-done.6.refs_3_ = f32[256,256]{1,0:T(8,128)} collective-permute-done((f32[256,256]{1,0:T(8,128)}, f32[256,256]{1,0:T(8,128)}, u32[]{:S(2)}, u32[]{:S(2)}) %collective-permute-start.6) | collective-permute-done | bytes 262176 | tf_op jit(solution)/shard_map/ppermute | solution.py:562
  125.0 6.9 %weigh_back.2 = (f32[2048,512]{1,0:T(8,128)}, f32[2048,256]{1,0:T(8,128)}) custom-call(s32[2]{0:T(128)} %pad_add_fusion.place, f32[256,256]{1,0:T(8,128)} %add_pieces.2.refs_0_, f32[256,256]{1,0:T(8,128)} %collective-permute-done.4.refs_1_, f32[256,256]{1,0:T(8,128)} %collective-permute-done.5.refs_2_, f32[256,256]{1,0:T(8,128)} %collective-permute-done.6.refs_3_, ...), custom_call_target="tpu_custom_call" | custom-call | flops 3000000000 | bytes 12582912 | tf_op jit(solution)/shard_map/weigh_back/pallas_call | solution.py:500
  131.9 4.6 %all-to-all-start.3 = ((f32[16,128,256]{2,1,0:T(8,128)}), f32[16,128,256]{2,1,0:T(8,128)}, u32[]{:S(2)}, u32[]{:S(2)}) async-start(f32[16,128,256]{2,1,0:T(8,128)} %bitcast.18), calls=%async_computation.3 | async-start | bytes 4194304 | tf_op jit(solution)/shard_map/all_to_all | solution.py:518
  136.5 2.3 %collective-permute-start.8 = (f32[256,256]{1,0:T(8,128)S(1)}, f32[256,256]{1,0:T(8,128)}, u32[]{:S(2)}, u32[]{:S(2)}) collective-permute-start(f32[256,256]{1,0:T(8,128)S(1)} %copy-done.9), channel_id=1, source_target_pairs={{0,32},{16,48},{32,64},{48,80},{64,96},{80,112},{96,0},{112,16},{1... | collective-permute-start | bytes 786440 | tf_op jit(solution)/shard_map/ppermute | solution.py:558
  139.4 5.1 %collective-permute-done.8.refs_1_ = f32[256,256]{1,0:T(8,128)} collective-permute-done((f32[256,256]{1,0:T(8,128)S(1)}, f32[256,256]{1,0:T(8,128)}, u32[]{:S(2)}, u32[]{:S(2)}) %collective-permute-start.8) | collective-permute-done | bytes 262176 | tf_op jit(solution)/shard_map/ppermute | solution.py:558
  144.5 3.1 %collective-permute-done.9.refs_2_ = f32[256,256]{1,0:T(8,128)} collective-permute-done((f32[256,256]{1,0:T(8,128)S(1)}, f32[256,256]{1,0:T(8,128)}, u32[]{:S(2)}, u32[]{:S(2)}) %collective-permute-start.9) | collective-permute-done | bytes 262176 | tf_op jit(solution)/shard_map/ppermute | solution.py:558
  147.7 6.1 %collective-permute-done.10.refs_3_ = f32[256,256]{1,0:T(8,128)} collective-permute-done((f32[256,256]{1,0:T(8,128)S(1)}, f32[256,256]{1,0:T(8,128)}, u32[]{:S(2)}, u32[]{:S(2)}) %collective-permute-start.10) | collective-permute-done | bytes 262176 | tf_op jit(solution)/shard_map/ppermute | solution.py:558
  159.9 10.2 %collective-permute-done.13.refs_3_ = f32[256,256]{1,0:T(8,128)S(1)} collective-permute-done((f32[256,256]{1,0:T(8,128)}, f32[256,256]{1,0:T(8,128)S(1)}, u32[]{:S(2)}, u32[]{:S(2)}) %collective-permute-start.13) | collective-permute-done | bytes 262176 | tf_op jit(solution)/shard_map/ppermute | solution.py:562
  175.3 6.9 %weigh_back.3 = (f32[2048,512]{1,0:T(8,128)}, f32[2048,256]{1,0:T(8,128)}) custom-call(s32[2]{0:T(128)} %pad_add_fusion.place, f32[256,256]{1,0:T(8,128)} %add_pieces.3.refs_0_, f32[256,256]{1,0:T(8,128)} %copy-done.2, f32[256,256]{1,0:T(8,128)} %copy-done.1, f32[256,256]{1,0:T(8,128)} %copy-done, ...), custom_call_target="tpu_custom_call", output_to_operand_aliasing={{0}: (11, {})} | custom-call | flops 3000000000 | bytes 12582912 | tf_op jit(solution)/shard_map/weigh_back/pallas_call | solution.py:500
  182.2 6.6 %all-to-all-start.2 = ((f32[16,128,256]{2,1,0:T(8,128)}), f32[16,128,256]{2,1,0:T(8,128)}, u32[]{:S(2)}, u32[]{:S(2)}) async-start(f32[16,128,256]{2,1,0:T(8,128)} %bitcast.20), calls=%async_computation.2 | async-start | bytes 4194304 | tf_op jit(solution)/shard_map/all_to_all | solution.py:518
  188.8 6.5 %column_back.2.rest_0_ = f32[2048,512]{1,0:T(8,128)} custom-call(f32[2048,256]{1,0:T(8,128)} %bitcast.14.x_ref, bf16[16,256,128]{2,1,0:T(8,128)(2,1)} %get-tuple-element.59.w_ref, bf16[2,8,2,256,256]{4,3,2,1,0:T(8,128)(2,1)} %get-tuple-element.60.g_ref), custom_call_target="tpu_custom_call" | custom-call | flops 4000000000 | bytes 9437184 | tf_op jit(solution)/shard_map/column_back/pallas_call | solution.py:318
  195.3 22.8 %all-to-all-done.2 = f32[16,128,256]{2,1,0:T(8,128)} async-done(((f32[16,128,256]{2,1,0:T(8,128)}), f32[16,128,256]{2,1,0:T(8,128)}, u32[]{:S(2)}, u32[]{:S(2)}) %all-to-all-start.2) | async-done | bytes 2097184 | tf_op jit(solution)/shard_map/all_to_all | solution.py:518
  218.2 6.5 %column_back.3 = f32[2048,512]{1,0:T(8,128)} custom-call(f32[2048,256]{1,0:T(8,128)} %bitcast.12.x_ref, bf16[16,256,128]{2,1,0:T(8,128)(2,1)} %get-tuple-element.59.w_ref, bf16[2,8,2,256,256]{4,3,2,1,0:T(8,128)(2,1)} %get-tuple-element.60.g_ref, f32[2048,512]{1,0:T(8,128)} %column_back.2.rest_0_), custom_call_target="tpu_custom_call", output_to_operand_aliasing={{}: (3, {})} | custom-call | flops 4000000000 | bytes 9437184 | tf_op jit(solution)/shard_map/column_back/pallas_call | solution.py:318
  (55 shorter events, 21.3 us)
Async XLA Ops:
  7.9 35.9 %all-to-all-start = ((f32[16,128,256]{2,1,0:T(8,128)}), f32[16,128,256]{2,1,0:T(8,128)}, u32[]{:S(2)}, u32[]{:S(2)}) async-start(f32[16,128,256]{2,1,0:T(8,128)} %bitcast.21), calls=%async_computation | async-start | bytes 4194304 | tf_op jit(solution)/shard_map/all_to_all | solution.py:518
  43.8 29.9 %all-to-all-start.1 = ((f32[16,128,256]{2,1,0:T(8,128)}), f32[16,128,256]{2,1,0:T(8,128)}, u32[]{:S(2)}, u32[]{:S(2)}) async-start(f32[16,128,256]{2,1,0:T(8,128)} %bitcast.19), calls=%async_computation.1 | async-start | bytes 4194304 | tf_op jit(solution)/shard_map/all_to_all | solution.py:518
  55.0 30.2 %collective-permute-start = (f32[1024,256]{1,0:T(8,128)}, f32[1024,256]{1,0:T(8,128)}, u32[]{:S(2)}, u32[]{:S(2)}) collective-permute-start(f32[1024,256]{1,0:T(8,128)} %get-tuple-element.34), channel_id=1, source_target_pairs={{0,16},{16,0},{32,48},{48,32},{64,80},{80,64},{96,112},{112,96},{1... | collective-permute-start | bytes 3145736 | tf_op jit(solution)/shard_map/ppermute | solution.py:548
  79.7 29.4 %collective-permute-start.7 = (f32[1024,256]{1,0:T(8,128)}, f32[1024,256]{1,0:T(8,128)}, u32[]{:S(2)}, u32[]{:S(2)}) collective-permute-start(f32[1024,256]{1,0:T(8,128)} %get-tuple-element.43), channel_id=1, source_target_pairs={{0,16},{16,0},{32,48},{48,32},{64,80},{80,64},{96,112},{112,96},{1... | collective-permute-start | bytes 3145736 | tf_op jit(solution)/shard_map/ppermute | solution.py:548
  88.3 8.2 %collective-permute-start.1 = (f32[256,256]{1,0:T(8,128)}, f32[256,256]{1,0:T(8,128)}, u32[]{:S(2)}, u32[]{:S(2)}) collective-permute-start(f32[256,256]{1,0:T(8,128)} %get-tuple-element.36), channel_id=1, source_target_pairs={{0,32},{16,48},{32,64},{48,80},{64,96},{80,112},{96,0},{112,16},{1... | collective-permute-start | bytes 786440 | tf_op jit(solution)/shard_map/ppermute | solution.py:558
  88.4 9.7 %collective-permute-start.2 = (f32[256,256]{1,0:T(8,128)}, f32[256,256]{1,0:T(8,128)}, u32[]{:S(2)}, u32[]{:S(2)}) collective-permute-start(f32[256,256]{1,0:T(8,128)} %get-tuple-element.37), channel_id=1, source_target_pairs={{0,64},{16,80},{32,96},{48,112},{64,0},{80,16},{96,32},{112,48},{1... | collective-permute-start | bytes 786440 | tf_op jit(solution)/shard_map/ppermute | solution.py:558
  90.6 13.5 %collective-permute-start.3 = (f32[256,256]{1,0:T(8,128)}, f32[256,256]{1,0:T(8,128)}, u32[]{:S(2)}, u32[]{:S(2)}) collective-permute-start(f32[256,256]{1,0:T(8,128)} %get-tuple-element.38), channel_id=1, source_target_pairs={{0,96},{16,112},{32,0},{48,16},{64,32},{80,48},{96,64},{112,80},{1... | collective-permute-start | bytes 786440 | tf_op jit(solution)/shard_map/ppermute | solution.py:558
  106.2 14.6 %collective-permute-start.6 = (f32[256,256]{1,0:T(8,128)}, f32[256,256]{1,0:T(8,128)}, u32[]{:S(2)}, u32[]{:S(2)}) collective-permute-start(f32[256,256]{1,0:T(8,128)} %add_pieces.2.refs_0_), channel_id=1, source_target_pairs={{0,96},{16,112},{32,0},{48,16},{64,32},{80,48},{96,64},{112,80},{1... | collective-permute-start | bytes 786440 | tf_op jit(solution)/shard_map/ppermute | solution.py:562
  106.3 14.5 %collective-permute-start.5 = (f32[256,256]{1,0:T(8,128)}, f32[256,256]{1,0:T(8,128)}, u32[]{:S(2)}, u32[]{:S(2)}) collective-permute-start(f32[256,256]{1,0:T(8,128)} %add_pieces.2.refs_0_), channel_id=1, source_target_pairs={{0,64},{16,80},{32,96},{48,112},{64,0},{80,16},{96,32},{112,48},{1... | collective-permute-start | bytes 786440 | tf_op jit(solution)/shard_map/ppermute | solution.py:562
  107.8 13.3 %collective-permute-start.4 = (f32[256,256]{1,0:T(8,128)}, f32[256,256]{1,0:T(8,128)}, u32[]{:S(2)}, u32[]{:S(2)}) collective-permute-start(f32[256,256]{1,0:T(8,128)} %add_pieces.2.refs_0_), channel_id=1, source_target_pairs={{0,32},{16,48},{32,64},{48,80},{64,96},{80,112},{96,0},{112,16},{1... | collective-permute-start | bytes 786440 | tf_op jit(solution)/shard_map/ppermute | solution.py:562
  112.1 11.1 %collective-permute-start.18 = (f32[256,256]{1,0:T(8,128)}, f32[256,256]{1,0:T(8,128)}, u32[]{:S(2)}, u32[]{:S(2)}) collective-permute-start(f32[256,256]{1,0:T(8,128)} %add_pieces.2.refs_0_), channel_id=1, source_target_pairs={{0,16},{16,0},{32,48},{48,32},{64,80},{80,64},{96,112},{112,96},{1... | collective-permute-start | bytes 786440 | tf_op jit(solution)/shard_map/ppermute | solution.py:566
  121.1 3.1 %collective-permute-start.19 = (f32[256,256]{1,0:T(8,128)}, f32[256,256]{1,0:T(8,128)}, u32[]{:S(2)}, u32[]{:S(2)}) collective-permute-start(f32[256,256]{1,0:T(8,128)} %collective-permute-done.4.refs_1_), channel_id=1, source_target_pairs={{0,16},{16,0},{32,48},{48,32},{64,80},{80,64},{96,112},{112,96},{1... | collective-permute-start | bytes 786440 | tf_op jit(solution)/shard_map/ppermute | solution.py:566
  122.7 1.9 collective-permute-start.20
  122.7 2.3 %collective-permute-start.21 = (f32[256,256]{1,0:T(8,128)}, f32[256,256]{1,0:T(8,128)}, u32[]{:S(2)}, u32[]{:S(2)}) collective-permute-start(f32[256,256]{1,0:T(8,128)} %collective-permute-done.6.refs_3_), channel_id=1, source_target_pairs={{0,16},{16,0},{32,48},{48,32},{64,80},{80,64},{96,112},{112,96},{1... | collective-permute-start | bytes 786440 | tf_op jit(solution)/shard_map/ppermute | solution.py:566
  131.8 4.6 %copy-start.9 = (f32[256,256]{1,0:T(8,128)S(1)}, f32[256,256]{1,0:T(8,128)}, u32[]{:S(2)}) copy-start(f32[256,256]{1,0:T(8,128)} %get-tuple-element.49) | copy-start | bytes 786436
  131.9 6.9 %copy-start.8 = (f32[256,256]{1,0:T(8,128)S(1)}, f32[256,256]{1,0:T(8,128)}, u32[]{:S(2)}) copy-start(f32[256,256]{1,0:T(8,128)} %get-tuple-element.50) | copy-start | bytes 786436
  131.9 6.9 %copy-start.7 = (f32[256,256]{1,0:T(8,128)S(1)}, f32[256,256]{1,0:T(8,128)}, u32[]{:S(2)}) copy-start(f32[256,256]{1,0:T(8,128)} %get-tuple-element.51) | copy-start | bytes 786436
  131.9 50.3 %all-to-all-start.3 = ((f32[16,128,256]{2,1,0:T(8,128)}), f32[16,128,256]{2,1,0:T(8,128)}, u32[]{:S(2)}, u32[]{:S(2)}) async-start(f32[16,128,256]{2,1,0:T(8,128)} %bitcast.18), calls=%async_computation.3 | async-start | bytes 4194304 | tf_op jit(solution)/shard_map/all_to_all | solution.py:518
  136.5 8.0 %collective-permute-start.8 = (f32[256,256]{1,0:T(8,128)S(1)}, f32[256,256]{1,0:T(8,128)}, u32[]{:S(2)}, u32[]{:S(2)}) collective-permute-start(f32[256,256]{1,0:T(8,128)S(1)} %copy-done.9), channel_id=1, source_target_pairs={{0,32},{16,48},{32,64},{48,80},{64,96},{80,112},{96,0},{112,16},{1... | collective-permute-start | bytes 786440 | tf_op jit(solution)/shard_map/ppermute | solution.py:558
  138.8 8.9 %collective-permute-start.9 = (f32[256,256]{1,0:T(8,128)S(1)}, f32[256,256]{1,0:T(8,128)}, u32[]{:S(2)}, u32[]{:S(2)}) collective-permute-start(f32[256,256]{1,0:T(8,128)S(1)} %copy-done.8), channel_id=1, source_target_pairs={{0,64},{16,80},{32,96},{48,112},{64,0},{80,16},{96,32},{112,48},{1... | collective-permute-start | bytes 786440 | tf_op jit(solution)/shard_map/ppermute | solution.py:558
  138.8 15.0 %collective-permute-start.10 = (f32[256,256]{1,0:T(8,128)S(1)}, f32[256,256]{1,0:T(8,128)}, u32[]{:S(2)}, u32[]{:S(2)}) collective-permute-start(f32[256,256]{1,0:T(8,128)S(1)} %copy-done.7), channel_id=1, source_target_pairs={{0,96},{16,112},{32,0},{48,16},{64,32},{80,48},{96,64},{112,80},{1... | collective-permute-start | bytes 786440 | tf_op jit(solution)/shard_map/ppermute | solution.py:558
  155.8 14.3 %collective-permute-start.13 = (f32[256,256]{1,0:T(8,128)}, f32[256,256]{1,0:T(8,128)S(1)}, u32[]{:S(2)}, u32[]{:S(2)}) collective-permute-start(f32[256,256]{1,0:T(8,128)} %add_pieces.3.refs_0_), channel_id=1, source_target_pairs={{0,96},{16,112},{32,0},{48,16},{64,32},{80,48},{96,64},{112,80},{1... | collective-permute-start | bytes 786440 | tf_op jit(solution)/shard_map/ppermute | solution.py:562
  155.9 16.4 %collective-permute-start.12 = (f32[256,256]{1,0:T(8,128)}, f32[256,256]{1,0:T(8,128)S(1)}, u32[]{:S(2)}, u32[]{:S(2)}) collective-permute-start(f32[256,256]{1,0:T(8,128)} %add_pieces.3.refs_0_), channel_id=1, source_target_pairs={{0,64},{16,80},{32,96},{48,112},{64,0},{80,16},{96,32},{112,48},{1... | collective-permute-start | bytes 786440 | tf_op jit(solution)/shard_map/ppermute | solution.py:562
  156.9 15.6 %collective-permute-start.11 = (f32[256,256]{1,0:T(8,128)}, f32[256,256]{1,0:T(8,128)S(1)}, u32[]{:S(2)}, u32[]{:S(2)}) collective-permute-start(f32[256,256]{1,0:T(8,128)} %add_pieces.3.refs_0_), channel_id=1, source_target_pairs={{0,32},{16,48},{32,64},{48,80},{64,96},{80,112},{96,0},{112,16},{1... | collective-permute-start | bytes 786440 | tf_op jit(solution)/shard_map/ppermute | solution.py:562
  158.6 14.3 %collective-permute-start.14 = (f32[256,256]{1,0:T(8,128)}, f32[256,256]{1,0:T(8,128)S(1)}, u32[]{:S(2)}, u32[]{:S(2)}) collective-permute-start(f32[256,256]{1,0:T(8,128)} %add_pieces.3.refs_0_), channel_id=1, source_target_pairs={{0,16},{16,0},{32,48},{48,32},{64,80},{80,64},{96,112},{112,96},{1... | collective-permute-start | bytes 786440 | tf_op jit(solution)/shard_map/ppermute | solution.py:566
  170.8 2.7 %collective-permute-start.17 = (f32[256,256]{1,0:T(8,128)S(1)}, f32[256,256]{1,0:T(8,128)S(1)}, u32[]{:S(2)}, u32[]{:S(2)}) collective-permute-start(f32[256,256]{1,0:T(8,128)S(1)} %collective-permute-done.13.refs_3_), channel_id=1, source_target_pairs={{0,16},{16,0},{32,48},{48,32},{64,80},{80,64},{96,112},{112,96},{1... | collective-permute-start | bytes 786440 | tf_op jit(solution)/shard_map/ppermute | solution.py:566
  172.4 1.2 copy-start.1
  172.4 1.5 collective-permute-start.16
  172.4 1.5 copy-start.2
  172.5 1.8 collective-permute-start.15
  172.9 1.4 copy-start.3
  182.2 35.9 %all-to-all-start.2 = ((f32[16,128,256]{2,1,0:T(8,128)}), f32[16,128,256]{2,1,0:T(8,128)}, u32[]{:S(2)}, u32[]{:S(2)}) async-start(f32[16,128,256]{2,1,0:T(8,128)} %bitcast.20), calls=%async_computation.2 | async-start | bytes 4194304 | tf_op jit(solution)/shard_map/all_to_all | solution.py:518
  (4 other events, 2.9 us)

commit v2 on v1

--- a/solution.py
+++ b/solution.py
@@ -11,6 +11,9 @@
 F32 = jnp.float32
 BF16 = jnp.bfloat16
 PARAMS = pltpu.CompilerParams(vmem_limit_bytes=67043328)
+ROW_PARAMS = pltpu.CompilerParams(vmem_limit_bytes=96 << 19)
+WEIGH_PARAMS = pltpu.CompilerParams(vmem_limit_bytes=112 << 19)
+SUM_PARAMS = pltpu.CompilerParams(vmem_limit_bytes=48 << 20)
 
 
 def split(value):
@@ -122,6 +125,7 @@
 
 SMEM0 = pl.BlockSpec(memory_space=pltpu.SMEM)
 HBM = pl.BlockSpec(memory_space=pltpu.HBM)
+ANYWHERE = pl.BlockSpec(memory_space=pl.ANY)
 SMEM = SMEM0
 
 
@@ -368,11 +372,11 @@
         functools.partial(row_kernel, first_bit, span),
         out_shape=(half, half),
         in_specs=[SMEM0, HBM, HBM],
-        out_specs=(HBM, HBM),
+        out_specs=(ANYWHERE, ANYWHERE),
         scratch_shapes=[pltpu.VMEM((rows, columns), F32), pltpu.VMEM(merged.shape, BF16), pltpu.VMEM((rows, columns), F32)]
         + [pltpu.VMEM(half.shape, F32)] * 2
         + [pltpu.SemaphoreType.DMA((32,))],
-        compiler_params=PARAMS,
+        compiler_params=ROW_PARAMS,
         cost_estimate=pl.CostEstimate(flops=3 * 10**9, transcendentals=0, bytes_accessed=8 << 20),
         name="row_tree",
     )(place, x, merged)
@@ -406,11 +410,11 @@
     return pl.pallas_call(
         functools.partial(add_halves_kernel, ring),
         out_shape=(piece,) * ring,
-        in_specs=[SMEM0, HBM, HBM],
-        out_specs=(HBM,) * ring,
+        in_specs=[SMEM0, ANYWHERE, ANYWHERE],
+        out_specs=(ANYWHERE,) * ring,
         scratch_shapes=[pltpu.VMEM((ring, size, columns), F32)] * 2
         + [pltpu.SemaphoreType.DMA((2, ring)), pltpu.SemaphoreType.DMA((ring,))],
-        compiler_params=PARAMS,
+        compiler_params=SUM_PARAMS,
         cost_estimate=pl.CostEstimate(flops=keep.size, transcendentals=0, bytes_accessed=12 * keep.size),
         name="add_halves",
     )(place, keep, got)
@@ -446,11 +450,11 @@
     return pl.pallas_call(
         functools.partial(add_pieces_kernel, count),
         out_shape=jax.ShapeDtypeStruct((rows, columns), F32),
-        in_specs=[HBM] * count,
-        out_specs=HBM,
+        in_specs=[ANYWHERE] * count,
+        out_specs=ANYWHERE,
         scratch_shapes=[pltpu.VMEM((count, parts, rows // parts, columns), F32)]
         + [pltpu.SemaphoreType.DMA((count, parts)), pltpu.SemaphoreType.DMA((parts,))],
-        compiler_params=PARAMS,
+        compiler_params=SUM_PARAMS,
         cost_estimate=pl.CostEstimate(flops=4 * pieces[0].size, transcendentals=0, bytes_accessed=20 * pieces[0].size),
         name="add_pieces",
     )(*pieces)
@@ -500,13 +504,13 @@
     return pl.pallas_call(
         functools.partial(weigh_kernel, first_bit, span, ring, chunk),
         out_shape=(jax.ShapeDtypeStruct((rows, total), F32), jax.ShapeDtypeStruct((rows, columns), F32)),
-        in_specs=[SMEM0] + [HBM] * (len(pieces) + 2 + len(extra)),
+        in_specs=[SMEM0] + [ANYWHERE] * len(pieces) + [HBM] * (2 + len(extra)),
         out_specs=(HBM, HBM),
         scratch_shapes=[pltpu.VMEM((rows, columns), F32), pltpu.VMEM(weights.shape, F32), pltpu.VMEM(merged.shape, BF16)]
         + [pltpu.VMEM((rows, columns), F32)] * 2
         + [pltpu.SemaphoreType.DMA((32,))],
         input_output_aliases={3 + len(pieces): 0} if extra else {},
-        compiler_params=PARAMS,
+        compiler_params=WEIGH_PARAMS,
         cost_estimate=pl.CostEstimate(flops=3 * 10**9, transcendentals=0, bytes_accessed=12 << 20),
         name="weigh_back",
     )(place, *pieces, weights, merged, *extra)

time: 228 us -> 227 us (level)
    pallas_call x2, Pallas kernels: 6 us -> 2.95 us  [add_halves(): pl.pallas_call(functools.partial(add_halves_kernel, ring), out_shape=(pie...]
    pallas_call x2, Pallas kernels: 12 us -> 14.5 us  [row_tree(): pl.pallas_call(functools.partial(row_kernel, first_bit, span), out_shape=...]
  transfers between devices with their start and end apart: 26 -> 26, of which waited for: 18 -> 18; matrix products, arithmetic and copies ran while one was open for 0% -> 0% of each run, Pallas kernels for 26% -> 25%
where the time goes in v2:
time: 227 us; the launch traced here: 222 us
  waiting for transfers between devices  92.8 us (41%)
  Pallas kernels  77.1 us (34%)
  starting transfers between devices  49.9 us (22%)
    all_to_all x4, waiting for transfers between devices, exchange(): lax.all_to_all(x.reshape(nodes, rows // nodes, columns), 'node', split_ax...  44.1 us
    ppermute x6, waiting for transfers between devices, shards(): got.append(lax.ppermute(pieces[d], 'block', shift[d]))  27.4 us
    all_to_all x4, starting transfers between devices, exchange(): lax.all_to_all(x.reshape(nodes, rows // nodes, columns), 'node', split_ax...  22.5 us
    pallas_call x3, Pallas kernels, merged_columns(): pl.pallas_call(functools.partial(merged_column_kernel, back, chunk), out_...  19.5 us
    ppermute x6, waiting for transfers between devices, shards(): mine.append(lax.ppermute(total_piece, 'block', shift[d]))  18.7 us
    pallas_call x2, Pallas kernels, row_tree(): pl.pallas_call(functools.partial(row_kernel, first_bit, span), out_shape=...  14.5 us
    pallas_call x2, Pallas kernels, weigh_back(): pl.pallas_call(functools.partial(weigh_kernel, first_bit, span, ring, chu...  13.8 us
    ppermute x2, starting transfers between devices, start(): got = lax.ppermute(halves[n][1], 'block', sibling)  8.89 us
  transfers between devices with their start and end apart: 26, of which 18 were waited for; matrix products, arithmetic and copies ran while one was open for 0% of the time, Pallas kernels for 25%

profile of v2, /device:TPU:25, one launch (start us, length us, event | category | flops | bytes accessed | tf_op | source)
XLA Modules:
  0.0 222.3 jit_solution(10398578018395298064)
XLA Ops:
  0.6 7.4 %column_tree.1 = f32[2048,256]{1,0:T(8,128)} custom-call(s32[5,1,32]{2,1,0:T(1,128)} %bitcast.26, f32[2048,512]{1,0:T(8,128)} %bitcast.23, f32[1,5,32,64,128]{4,3,2,1,0:T(8,128)} %fe_ref.1), custom_call_target="tpu_custom_call" | custom-call | flops 5000000000 | bytes 9437184 | tf_op jit(solution)/shard_map/column_tree/pallas_call | solution.py:112
  8.0 7.7 %all-to-all-start = ((f32[16,128,256]{2,1,0:T(8,128)}), f32[16,128,256]{2,1,0:T(8,128)}, u32[]{:S(2)}, u32[]{:S(2)}) async-start(f32[16,128,256]{2,1,0:T(8,128)} %bitcast.22), calls=%async_computation | async-start | bytes 4194304 | tf_op jit(solution)/shard_map/all_to_all | solution.py:522
  15.7 8.0 %merge_columns.1 = (bf16[16,256,128]{2,1,0:T(8,128)(2,1)}, bf16[16,256,128]{2,1,0:T(8,128)(2,1)}, bf16[2,8,2,256,256]{4,3,2,1,0:T(8,128)(2,1)}, bf16[2,8,2,256,256]{4,3,2,1,0:T(8,128)(2,1)}) custom-call(s32[5,1,32]{2,1,0:T(1,128)} %bitcast.27, f32[1,5,32,64,128]{4,3,2,1,0:T(8,128)} %fe_ref.1, f32[1,5,32,64,128]{4,3,2,1,0:T(8,128)} %fe_ref.1, ...), custom_call_target="tpu_custom_call" | custom-call | flops 10000000000 | bytes 15728640 | tf_op jit(solution)/shard_map/merge_columns/pallas_call | solution.py:215
  23.7 7.4 %merge_rows.1 = (f32[2048,128]{1,0:T(8,128)}, bf16[2,8,2,256,256]{4,3,2,1,0:T(8,128)(2,1)}, bf16[2,8,2,256,256]{4,3,2,1,0:T(8,128)(2,1)}) custom-call(s32[4,1,32]{2,1,0:T(1,128)} %bitcast.28, f32[1,4,32,64,128]{4,3,2,1,0:T(8,128)} %fb_ref.2, f32[1,4,32,64,128]{4,3,2,1,0:T(8,128)} %fb_ref.2, f32[16,128]{1,0:T(8,128)} %bitcast.25), custom_call_target="tpu_custom_call" | custom-call | flops 10000000000 | bytes 12582912 | tf_op jit(solution)/shard_map/merge_rows/pallas_call | solution.py:232
  31.1 6.5 %column_tree_merged.1 = f32[2048,256]{1,0:T(8,128)} custom-call(f32[2048,512]{1,0:T(8,128)} %bitcast.24, bf16[16,256,128]{2,1,0:T(8,128)(2,1)} %get-tuple-element.39.w_ref, bf16[2,8,2,256,256]{4,3,2,1,0:T(8,128)(2,1)} %get-tuple-element.40.g_ref, f32[2048,128]{1,0:T(8,128)} %get-tuple-element.41.rest_0_.refs_8_), custom_call_target="tpu_custom_call" | custom-call | flops 4000000000 | bytes 9437184 | tf_op jit(solution)/shard_map/column_tree_merged/pallas_call | solution.py:322
  37.6 6.3 %all-to-all-done = f32[16,128,256]{2,1,0:T(8,128)} async-done(((f32[16,128,256]{2,1,0:T(8,128)}), f32[16,128,256]{2,1,0:T(8,128)}, u32[]{:S(2)}, u32[]{:S(2)}) %all-to-all-start) | async-done | bytes 2097184 | tf_op jit(solution)/shard_map/all_to_all | solution.py:522
  43.9 3.9 %all-to-all-start.1 = ((f32[16,128,256]{2,1,0:T(8,128)}), f32[16,128,256]{2,1,0:T(8,128)S(1)}, u32[]{:S(2)}, u32[]{:S(2)}) async-start(f32[16,128,256]{2,1,0:T(8,128)} %bitcast.20), calls=%async_computation.1 | async-start | bytes 4194304 | tf_op jit(solution)/shard_map/all_to_all | solution.py:522
  47.9 6.9 %row_tree.2 = (f32[1024,256]{1,0:T(8,128)S(1)}, f32[1024,256]{1,0:T(8,128)}) custom-call(s32[2]{0:T(128)S(1)} %pad_add_fusion.place, f32[2048,256]{1,0:T(8,128)} %bitcast.5.x_ref, bf16[2,8,2,256,256]{4,3,2,1,0:T(8,128)(2,1)} %get-tuple-element.32.g_ref), custom_call_target="tpu_custom_call" | custom-call | flops 3000000000 | bytes 8388608 | tf_op jit(solution)/shard_map/row_tree/pallas_call | solution.py:371
  54.8 3.3 %collective-permute-start = (f32[1024,256]{1,0:T(8,128)}, f32[1024,256]{1,0:T(8,128)}, u32[]{:S(2)}, u32[]{:S(2)}) collective-permute-start(f32[1024,256]{1,0:T(8,128)} %get-tuple-element.34), channel_id=1, source_target_pairs={{0,16},{16,0},{32,48},{48,32},{64,80},{80,64},{96,112},{112,96},{1... | collective-permute-start | bytes 3145736 | tf_op jit(solution)/shard_map/ppermute | solution.py:552
  58.1 14.9 %all-to-all-done.1 = f32[16,128,256]{2,1,0:T(8,128)S(1)} async-done(((f32[16,128,256]{2,1,0:T(8,128)}), f32[16,128,256]{2,1,0:T(8,128)S(1)}, u32[]{:S(2)}, u32[]{:S(2)}) %all-to-all-start.1) | async-done | bytes 2097184 | tf_op jit(solution)/shard_map/all_to_all | solution.py:522
  73.0 7.6 %row_tree.3 = (f32[1024,256]{1,0:T(8,128)S(1)}, f32[1024,256]{1,0:T(8,128)S(1)}) custom-call(s32[2]{0:T(128)S(1)} %pad_add_fusion.place, f32[2048,256]{1,0:T(8,128)S(1)} %bitcast.17, bf16[2,8,2,256,256]{4,3,2,1,0:T(8,128)(2,1)} %get-tuple-element.32.g_ref), custom_call_target="tpu_custom_call" | custom-call | flops 3000000000 | bytes 8388608 | tf_op jit(solution)/shard_map/row_tree/pallas_call | solution.py:371
  80.7 5.6 %collective-permute-start.7 = (f32[1024,256]{1,0:T(8,128)S(1)}, f32[1024,256]{1,0:T(8,128)S(1)}, u32[]{:S(2)}, u32[]{:S(2)}) collective-permute-start(f32[1024,256]{1,0:T(8,128)S(1)} %get-tuple-element.43), channel_id=1, source_target_pairs={{0,16},{16,0},{32,48},{48,32},{64,80},{80,64},{96,112},{112,96},{1... | collective-permute-start | bytes 3145736 | tf_op jit(solution)/shard_map/ppermute | solution.py:552
  86.3 1.9 add_halves.2
  88.3 2.2 %collective-permute-start.2 = (f32[256,256]{1,0:T(8,128)S(1)}, f32[256,256]{1,0:T(8,128)S(1)}, u32[]{:S(2)}, u32[]{:S(2)}) collective-permute-start(f32[256,256]{1,0:T(8,128)S(1)} %get-tuple-element.37), channel_id=1, source_target_pairs={{0,64},{16,80},{32,96},{48,112},{64,0},{80,16},{96,32},{112,48},{1... | collective-permute-start | bytes 786440 | tf_op jit(solution)/shard_map/ppermute | solution.py:562
  90.5 5.6 %collective-permute-done.1.refs_1_ = f32[256,256]{1,0:T(8,128)S(1)} collective-permute-done((f32[256,256]{1,0:T(8,128)S(1)}, f32[256,256]{1,0:T(8,128)S(1)}, u32[]{:S(2)}, u32[]{:S(2)}) %collective-permute-start.1) | collective-permute-done | bytes 262176 | tf_op jit(solution)/shard_map/ppermute | solution.py:562
  97.7 6.0 %collective-permute-done.3.refs_3_ = f32[256,256]{1,0:T(8,128)S(1)} collective-permute-done((f32[256,256]{1,0:T(8,128)S(1)}, f32[256,256]{1,0:T(8,128)S(1)}, u32[]{:S(2)}, u32[]{:S(2)}) %collective-permute-start.3) | collective-permute-done | bytes 262176 | tf_op jit(solution)/shard_map/ppermute | solution.py:562
  103.7 1.8 add_pieces.2.refs_0_
  109.5 2.1 collective-permute-start.18
  111.6 8.2 %collective-permute-done.6.refs_3_ = f32[256,256]{1,0:T(8,128)S(1)} collective-permute-done((f32[256,256]{1,0:T(8,128)S(1)}, f32[256,256]{1,0:T(8,128)S(1)}, u32[]{:S(2)}, u32[]{:S(2)}) %collective-permute-start.6) | collective-permute-done | bytes 262176 | tf_op jit(solution)/shard_map/ppermute | solution.py:566
  124.4 6.8 %weigh_back.2 = (f32[2048,512]{1,0:T(8,128)}, f32[2048,256]{1,0:T(8,128)}) custom-call(s32[2]{0:T(128)} %copy-done.2, f32[256,256]{1,0:T(8,128)} %copy-done.1, f32[256,256]{1,0:T(8,128)} %copy-done.12, f32[256,256]{1,0:T(8,128)} %copy-done.11, f32[256,256]{1,0:T(8,128)} %copy-done.10, f32[256,256]{1,0:T(8,128)} %copy-done.13, f32[256,256]{1,0:T(8,128)} %copy-done.14, ...), custom_call_target="tpu_custom_call" | custom-call | flops 3000000000 | bytes 12582912 | tf_op jit(solution)/shard_map/weigh_back/pallas_call | solution.py:504
  131.3 4.5 %all-to-all-start.3 = ((f32[16,128,256]{2,1,0:T(8,128)}), f32[16,128,256]{2,1,0:T(8,128)}, u32[]{:S(2)}, u32[]{:S(2)}) async-start(f32[16,128,256]{2,1,0:T(8,128)} %bitcast.19), calls=%async_computation.3 | async-start | bytes 4194304 | tf_op jit(solution)/shard_map/all_to_all | solution.py:522
  135.7 2.3 %collective-permute-start.8 = (f32[256,256]{1,0:T(8,128)S(1)}, f32[256,256]{1,0:T(8,128)S(1)}, u32[]{:S(2)}, u32[]{:S(2)}) collective-permute-start(f32[256,256]{1,0:T(8,128)S(1)} %get-tuple-element.49), channel_id=1, source_target_pairs={{0,32},{16,48},{32,64},{48,80},{64,96},{80,112},{96,0},{112,16},{1... | collective-permute-start | bytes 786440 | tf_op jit(solution)/shard_map/ppermute | solution.py:562
  138.7 5.2 %collective-permute-done.8.refs_1_ = f32[256,256]{1,0:T(8,128)S(1)} collective-permute-done((f32[256,256]{1,0:T(8,128)S(1)}, f32[256,256]{1,0:T(8,128)S(1)}, u32[]{:S(2)}, u32[]{:S(2)}) %collective-permute-start.8) | collective-permute-done | bytes 262176 | tf_op jit(solution)/shard_map/ppermute | solution.py:562
  143.9 3.1 %collective-permute-done.9.refs_2_ = f32[256,256]{1,0:T(8,128)S(1)} collective-permute-done((f32[256,256]{1,0:T(8,128)S(1)}, f32[256,256]{1,0:T(8,128)S(1)}, u32[]{:S(2)}, u32[]{:S(2)}) %collective-permute-start.9) | collective-permute-done | bytes 262176 | tf_op jit(solution)/shard_map/ppermute | solution.py:562
  147.0 6.0 %collective-permute-done.10.refs_3_ = f32[256,256]{1,0:T(8,128)S(1)} collective-permute-done((f32[256,256]{1,0:T(8,128)S(1)}, f32[256,256]{1,0:T(8,128)S(1)}, u32[]{:S(2)}, u32[]{:S(2)}) %collective-permute-start.10) | collective-permute-done | bytes 262176 | tf_op jit(solution)/shard_map/ppermute | solution.py:562
  152.9 1.8 add_pieces.3.refs_0_
  158.7 10.1 %collective-permute-done.13.refs_3_ = f32[256,256]{1,0:T(8,128)S(1)} collective-permute-done((f32[256,256]{1,0:T(8,128)S(1)}, f32[256,256]{1,0:T(8,128)S(1)}, u32[]{:S(2)}, u32[]{:S(2)}) %collective-permute-start.13) | collective-permute-done | bytes 262176 | tf_op jit(solution)/shard_map/ppermute | solution.py:566
  173.0 6.9 %weigh_back.3 = (f32[2048,512]{1,0:T(8,128)}, f32[2048,256]{1,0:T(8,128)}) custom-call(s32[2]{0:T(128)} %copy-done.2, f32[256,256]{1,0:T(8,128)} %copy-done, f32[256,256]{1,0:T(8,128)} %copy-done.5, f32[256,256]{1,0:T(8,128)} %copy-done.4, f32[256,256]{1,0:T(8,128)} %copy-done.3, f32[256,256]{1,0:T(8,128)} %copy-done.6, ...), custom_call_target="tpu_custom_call", output_to_operand_aliasing={{0}: (11, {})} | custom-call | flops 3000000000 | bytes 12582912 | tf_op jit(solution)/shard_map/weigh_back/pallas_call | solution.py:504
  179.9 6.4 %all-to-all-start.2 = ((f32[16,128,256]{2,1,0:T(8,128)}), f32[16,128,256]{2,1,0:T(8,128)}, u32[]{:S(2)}, u32[]{:S(2)}) async-start(f32[16,128,256]{2,1,0:T(8,128)} %bitcast.21), calls=%async_computation.2 | async-start | bytes 4194304 | tf_op jit(solution)/shard_map/all_to_all | solution.py:522
  186.4 6.5 %column_back.2.rest_0_ = f32[2048,512]{1,0:T(8,128)} custom-call(f32[2048,256]{1,0:T(8,128)} %bitcast.14.x_ref, bf16[16,256,128]{2,1,0:T(8,128)(2,1)} %get-tuple-element.59.w_ref, bf16[2,8,2,256,256]{4,3,2,1,0:T(8,128)(2,1)} %get-tuple-element.60.g_ref), custom_call_target="tpu_custom_call" | custom-call | flops 4000000000 | bytes 9437184 | tf_op jit(solution)/shard_map/column_back/pallas_call | solution.py:322
  192.8 22.8 %all-to-all-done.2 = f32[16,128,256]{2,1,0:T(8,128)} async-done(((f32[16,128,256]{2,1,0:T(8,128)}), f32[16,128,256]{2,1,0:T(8,128)}, u32[]{:S(2)}, u32[]{:S(2)}) %all-to-all-start.2) | async-done | bytes 2097184 | tf_op jit(solution)/shard_map/all_to_all | solution.py:522
  215.7 6.5 %column_back.3 = f32[2048,512]{1,0:T(8,128)} custom-call(f32[2048,256]{1,0:T(8,128)} %bitcast.12.x_ref, bf16[16,256,128]{2,1,0:T(8,128)(2,1)} %get-tuple-element.59.w_ref, bf16[2,8,2,256,256]{4,3,2,1,0:T(8,128)(2,1)} %get-tuple-element.60.g_ref, f32[2048,512]{1,0:T(8,128)} %column_back.2.rest_0_), custom_call_target="tpu_custom_call", output_to_operand_aliasing={{}: (3, {})} | custom-call | flops 4000000000 | bytes 9437184 | tf_op jit(solution)/shard_map/column_back/pallas_call | solution.py:322
  (69 shorter events, 19.0 us)
Async XLA Ops:
  8.0 35.9 %all-to-all-start = ((f32[16,128,256]{2,1,0:T(8,128)}), f32[16,128,256]{2,1,0:T(8,128)}, u32[]{:S(2)}, u32[]{:S(2)}) async-start(f32[16,128,256]{2,1,0:T(8,128)} %bitcast.22), calls=%async_computation | async-start | bytes 4194304 | tf_op jit(solution)/shard_map/all_to_all | solution.py:522
  43.9 29.1 %all-to-all-start.1 = ((f32[16,128,256]{2,1,0:T(8,128)}), f32[16,128,256]{2,1,0:T(8,128)S(1)}, u32[]{:S(2)}, u32[]{:S(2)}) async-start(f32[16,128,256]{2,1,0:T(8,128)} %bitcast.20), calls=%async_computation.1 | async-start | bytes 4194304 | tf_op jit(solution)/shard_map/all_to_all | solution.py:522
  47.9 60.6 %copy-start.2 = (s32[2]{0:T(128)}, s32[2]{0:T(128)S(1)}, u32[]{:S(2)}) copy-start(s32[2]{0:T(128)S(1)} %pad_add_fusion.place) | copy-start | bytes 28
  54.8 31.5 %collective-permute-start = (f32[1024,256]{1,0:T(8,128)}, f32[1024,256]{1,0:T(8,128)}, u32[]{:S(2)}, u32[]{:S(2)}) collective-permute-start(f32[1024,256]{1,0:T(8,128)} %get-tuple-element.34), channel_id=1, source_target_pairs={{0,16},{16,0},{32,48},{48,32},{64,80},{80,64},{96,112},{112,96},{1... | collective-permute-start | bytes 3145736 | tf_op jit(solution)/shard_map/ppermute | solution.py:552
  80.7 27.8 %collective-permute-start.7 = (f32[1024,256]{1,0:T(8,128)S(1)}, f32[1024,256]{1,0:T(8,128)S(1)}, u32[]{:S(2)}, u32[]{:S(2)}) collective-permute-start(f32[1024,256]{1,0:T(8,128)S(1)} %get-tuple-element.43), channel_id=1, source_target_pairs={{0,16},{16,0},{32,48},{48,32},{64,80},{80,64},{96,112},{112,96},{1... | collective-permute-start | bytes 3145736 | tf_op jit(solution)/shard_map/ppermute | solution.py:552
  88.2 7.9 %collective-permute-start.1 = (f32[256,256]{1,0:T(8,128)S(1)}, f32[256,256]{1,0:T(8,128)S(1)}, u32[]{:S(2)}, u32[]{:S(2)}) collective-permute-start(f32[256,256]{1,0:T(8,128)S(1)} %get-tuple-element.36), channel_id=1, source_target_pairs={{0,32},{16,48},{32,64},{48,80},{64,96},{80,112},{96,0},{112,16},{1... | collective-permute-start | bytes 786440 | tf_op jit(solution)/shard_map/ppermute | solution.py:562
  88.3 9.4 %collective-permute-start.2 = (f32[256,256]{1,0:T(8,128)S(1)}, f32[256,256]{1,0:T(8,128)S(1)}, u32[]{:S(2)}, u32[]{:S(2)}) collective-permute-start(f32[256,256]{1,0:T(8,128)S(1)} %get-tuple-element.37), channel_id=1, source_target_pairs={{0,64},{16,80},{32,96},{48,112},{64,0},{80,16},{96,32},{112,48},{1... | collective-permute-start | bytes 786440 | tf_op jit(solution)/shard_map/ppermute | solution.py:562
  90.5 13.2 %collective-permute-start.3 = (f32[256,256]{1,0:T(8,128)S(1)}, f32[256,256]{1,0:T(8,128)S(1)}, u32[]{:S(2)}, u32[]{:S(2)}) collective-permute-start(f32[256,256]{1,0:T(8,128)S(1)} %get-tuple-element.38), channel_id=1, source_target_pairs={{0,96},{16,112},{32,0},{48,16},{64,32},{80,48},{96,64},{112,80},{1... | collective-permute-start | bytes 786440 | tf_op jit(solution)/shard_map/ppermute | solution.py:562
  105.5 18.2 %copy-start.1 = (f32[256,256]{1,0:T(8,128)}, f32[256,256]{1,0:T(8,128)S(1)}, u32[]{:S(2)}) copy-start(f32[256,256]{1,0:T(8,128)S(1)} %add_pieces.2.refs_0_) | copy-start | bytes 786436
  105.5 14.3 %collective-permute-start.6 = (f32[256,256]{1,0:T(8,128)S(1)}, f32[256,256]{1,0:T(8,128)S(1)}, u32[]{:S(2)}, u32[]{:S(2)}) collective-permute-start(f32[256,256]{1,0:T(8,128)S(1)} %add_pieces.2.refs_0_), channel_id=1, source_target_pairs={{0,96},{16,112},{32,0},{48,16},{64,32},{80,48},{96,64},{112,80},{1... | collective-permute-start | bytes 786440 | tf_op jit(solution)/shard_map/ppermute | solution.py:566
  105.7 14.2 %collective-permute-start.5 = (f32[256,256]{1,0:T(8,128)S(1)}, f32[256,256]{1,0:T(8,128)S(1)}, u32[]{:S(2)}, u32[]{:S(2)}) collective-permute-start(f32[256,256]{1,0:T(8,128)S(1)} %add_pieces.2.refs_0_), channel_id=1, source_target_pairs={{0,64},{16,80},{32,96},{48,112},{64,0},{80,16},{96,32},{112,48},{1... | collective-permute-start | bytes 786440 | tf_op jit(solution)/shard_map/ppermute | solution.py:566
  107.2 13.0 %collective-permute-start.4 = (f32[256,256]{1,0:T(8,128)S(1)}, f32[256,256]{1,0:T(8,128)S(1)}, u32[]{:S(2)}, u32[]{:S(2)}) collective-permute-start(f32[256,256]{1,0:T(8,128)S(1)} %add_pieces.2.refs_0_), channel_id=1, source_target_pairs={{0,32},{16,48},{32,64},{48,80},{64,96},{80,112},{96,0},{112,16},{1... | collective-permute-start | bytes 786440 | tf_op jit(solution)/shard_map/ppermute | solution.py:566
  109.5 12.8 %collective-permute-start.18 = (f32[256,256]{1,0:T(8,128)S(1)}, f32[256,256]{1,0:T(8,128)S(1)}, u32[]{:S(2)}, u32[]{:S(2)}) collective-permute-start(f32[256,256]{1,0:T(8,128)S(1)} %add_pieces.2.refs_0_), channel_id=1, source_target_pairs={{0,16},{16,0},{32,48},{48,32},{64,80},{80,64},{96,112},{112,96},{1... | collective-permute-start | bytes 786440 | tf_op jit(solution)/shard_map/ppermute | solution.py:570
  119.8 3.9 %copy-start.10 = (f32[256,256]{1,0:T(8,128)}, f32[256,256]{1,0:T(8,128)S(1)}, u32[]{:S(2)}) copy-start(f32[256,256]{1,0:T(8,128)S(1)} %collective-permute-done.6.refs_3_) | copy-start | bytes 786436
  119.8 3.9 %copy-start.11 = (f32[256,256]{1,0:T(8,128)}, f32[256,256]{1,0:T(8,128)S(1)}, u32[]{:S(2)}) copy-start(f32[256,256]{1,0:T(8,128)S(1)} %collective-permute-done.5.refs_2_) | copy-start | bytes 786436
  120.2 3.5 %copy-start.12 = (f32[256,256]{1,0:T(8,128)}, f32[256,256]{1,0:T(8,128)S(1)}, u32[]{:S(2)}) copy-start(f32[256,256]{1,0:T(8,128)S(1)} %collective-permute-done.4.refs_1_) | copy-start | bytes 786436
  120.2 2.7 %collective-permute-start.19 = (f32[256,256]{1,0:T(8,128)S(1)}, f32[256,256]{1,0:T(8,128)S(1)}, u32[]{:S(2)}, u32[]{:S(2)}) collective-permute-start(f32[256,256]{1,0:T(8,128)S(1)} %collective-permute-done.4.refs_1_), channel_id=1, source_target_pairs={{0,16},{16,0},{32,48},{48,32},{64,80},{80,64},{96,112},{112,96},{1... | collective-permute-start | bytes 786440 | tf_op jit(solution)/shard_map/ppermute | solution.py:570
  121.8 1.5 collective-permute-start.20
  121.8 1.9 collective-permute-start.21
  131.3 48.6 %all-to-all-start.3 = ((f32[16,128,256]{2,1,0:T(8,128)}), f32[16,128,256]{2,1,0:T(8,128)}, u32[]{:S(2)}, u32[]{:S(2)}) async-start(f32[16,128,256]{2,1,0:T(8,128)} %bitcast.19), calls=%async_computation.3 | async-start | bytes 4194304 | tf_op jit(solution)/shard_map/all_to_all | solution.py:522
  135.7 8.2 %collective-permute-start.8 = (f32[256,256]{1,0:T(8,128)S(1)}, f32[256,256]{1,0:T(8,128)S(1)}, u32[]{:S(2)}, u32[]{:S(2)}) collective-permute-start(f32[256,256]{1,0:T(8,128)S(1)} %get-tuple-element.49), channel_id=1, source_target_pairs={{0,32},{16,48},{32,64},{48,80},{64,96},{80,112},{96,0},{112,16},{1... | collective-permute-start | bytes 786440 | tf_op jit(solution)/shard_map/ppermute | solution.py:562
  138.0 8.9 %collective-permute-start.9 = (f32[256,256]{1,0:T(8,128)S(1)}, f32[256,256]{1,0:T(8,128)S(1)}, u32[]{:S(2)}, u32[]{:S(2)}) collective-permute-start(f32[256,256]{1,0:T(8,128)S(1)} %get-tuple-element.50), channel_id=1, source_target_pairs={{0,64},{16,80},{32,96},{48,112},{64,0},{80,16},{96,32},{112,48},{1... | collective-permute-start | bytes 786440 | tf_op jit(solution)/shard_map/ppermute | solution.py:562
  138.0 14.9 %collective-permute-start.10 = (f32[256,256]{1,0:T(8,128)S(1)}, f32[256,256]{1,0:T(8,128)S(1)}, u32[]{:S(2)}, u32[]{:S(2)}) collective-permute-start(f32[256,256]{1,0:T(8,128)S(1)} %get-tuple-element.51), channel_id=1, source_target_pairs={{0,96},{16,112},{32,0},{48,16},{64,32},{80,48},{96,64},{112,80},{1... | collective-permute-start | bytes 786440 | tf_op jit(solution)/shard_map/ppermute | solution.py:562
  154.7 17.6 %copy-start = (f32[256,256]{1,0:T(8,128)}, f32[256,256]{1,0:T(8,128)S(1)}, u32[]{:S(2)}) copy-start(f32[256,256]{1,0:T(8,128)S(1)} %add_pieces.3.refs_0_) | copy-start | bytes 786436
  154.7 14.1 %collective-permute-start.13 = (f32[256,256]{1,0:T(8,128)S(1)}, f32[256,256]{1,0:T(8,128)S(1)}, u32[]{:S(2)}, u32[]{:S(2)}) collective-permute-start(f32[256,256]{1,0:T(8,128)S(1)} %add_pieces.3.refs_0_), channel_id=1, source_target_pairs={{0,96},{16,112},{32,0},{48,16},{64,32},{80,48},{96,64},{112,80},{1... | collective-permute-start | bytes 786440 | tf_op jit(solution)/shard_map/ppermute | solution.py:566
  154.8 15.5 %collective-permute-start.12 = (f32[256,256]{1,0:T(8,128)S(1)}, f32[256,256]{1,0:T(8,128)S(1)}, u32[]{:S(2)}, u32[]{:S(2)}) collective-permute-start(f32[256,256]{1,0:T(8,128)S(1)} %add_pieces.3.refs_0_), channel_id=1, source_target_pairs={{0,64},{16,80},{32,96},{48,112},{64,0},{80,16},{96,32},{112,48},{1... | collective-permute-start | bytes 786440 | tf_op jit(solution)/shard_map/ppermute | solution.py:566
  155.9 14.5 %collective-permute-start.11 = (f32[256,256]{1,0:T(8,128)S(1)}, f32[256,256]{1,0:T(8,128)S(1)}, u32[]{:S(2)}, u32[]{:S(2)}) collective-permute-start(f32[256,256]{1,0:T(8,128)S(1)} %add_pieces.3.refs_0_), channel_id=1, source_target_pairs={{0,32},{16,48},{32,64},{48,80},{64,96},{80,112},{96,0},{112,16},{1... | collective-permute-start | bytes 786440 | tf_op jit(solution)/shard_map/ppermute | solution.py:566
  157.5 13.5 %collective-permute-start.14 = (f32[256,256]{1,0:T(8,128)S(1)}, f32[256,256]{1,0:T(8,128)S(1)}, u32[]{:S(2)}, u32[]{:S(2)}) collective-permute-start(f32[256,256]{1,0:T(8,128)S(1)} %add_pieces.3.refs_0_), channel_id=1, source_target_pairs={{0,16},{16,0},{32,48},{48,32},{64,80},{80,64},{96,112},{112,96},{1... | collective-permute-start | bytes 786440 | tf_op jit(solution)/shard_map/ppermute | solution.py:570
  168.8 2.7 %collective-permute-start.17 = (f32[256,256]{1,0:T(8,128)S(1)}, f32[256,256]{1,0:T(8,128)S(1)}, u32[]{:S(2)}, u32[]{:S(2)}) collective-permute-start(f32[256,256]{1,0:T(8,128)S(1)} %collective-permute-done.13.refs_3_), channel_id=1, source_target_pairs={{0,16},{16,0},{32,48},{48,32},{64,80},{80,64},{96,112},{112,96},{1... | collective-permute-start | bytes 786440 | tf_op jit(solution)/shard_map/ppermute | solution.py:570
  170.4 1.5 collective-permute-start.16
  170.5 1.8 collective-permute-start.15
  179.9 35.7 %all-to-all-start.2 = ((f32[16,128,256]{2,1,0:T(8,128)}), f32[16,128,256]{2,1,0:T(8,128)}, u32[]{:S(2)}, u32[]{:S(2)}) async-start(f32[16,128,256]{2,1,0:T(8,128)} %bitcast.21), calls=%async_computation.2 | async-start | bytes 4194304 | tf_op jit(solution)/shard_map/all_to_all | solution.py:522
  (11 other events, 14.4 us)

commit v3 on v2

--- a/solution.py
+++ b/solution.py
@@ -126,6 +126,7 @@
 SMEM0 = pl.BlockSpec(memory_space=pltpu.SMEM)
 HBM = pl.BlockSpec(memory_space=pltpu.HBM)
 ANYWHERE = pl.BlockSpec(memory_space=pl.ANY)
+VMEM = pl.BlockSpec(memory_space=pltpu.VMEM)
 SMEM = SMEM0
 
 
@@ -334,12 +335,12 @@
     )(x, single, merged, *extra)
 
 
-def row_kernel(first_bit, span, place, x_ref, g_ref, keep_ref, send_ref, x_buf, g_buf, buf, keep_buf, send_buf, sems):
+def row_kernel(first_bit, span, place, x_ref, g_ref, keep_ref, send_ref, x_buf, g_buf, buf, sems):
     swap = place[1] == 1
     rows = x_buf.shape[0]
     copies = Copies(sems)
     size = g_buf.shape[1] // PARTS
-    entry, outs = [], []
+    entry = []
     for p in range(PARTS):
         r = part_rows(rows, 1)[p][0]
         g_part = copies.start(g_ref.at[0, pl.ds(p * size, size)], g_buf.at[0, pl.ds(p * size, size)])
@@ -349,20 +350,14 @@
     def store(quad, value):
         half = 2 * span
         low, high = value[:half], value[half:]
-        put(keep_buf, quad[:2], span, jnp.where(swap, high, low))
-        put(send_buf, quad[:2], span, jnp.where(swap, low, high))
-
-    def leave(p):
-        for r in part_rows(rows // 2, 2)[p]:
-            outs.append(copies.start(send_buf.at[r], send_ref.at[r]))
-            outs.append(copies.start(keep_buf.at[r], keep_ref.at[r]))
+        put(keep_ref, quad[:2], span, jnp.where(swap, high, low))
+        put(send_ref, quad[:2], span, jnp.where(swap, low, high))
 
     load = lambda ref: lambda quad: take(ref, quad, span)
     quad_stage(
         g_buf, 0, first_bit, load(x_buf), lambda quad, value: put(buf, quad, span, value), lambda p: wait_all(entry[p])
     )
-    quad_stage(g_buf, 1, first_bit + 2, load(buf), store, lambda p: g_copies[p].wait(), leave)
-    wait_all(outs)
+    quad_stage(g_buf, 1, first_bit + 2, load(buf), store, lambda p: g_copies[p].wait())
 
 
 def row_tree(x, merged, place, first_bit, span):
@@ -372,9 +367,8 @@
         functools.partial(row_kernel, first_bit, span),
         out_shape=(half, half),
         in_specs=[SMEM0, HBM, HBM],
-        out_specs=(ANYWHERE, ANYWHERE),
+        out_specs=(VMEM, VMEM),
         scratch_shapes=[pltpu.VMEM((rows, columns), F32), pltpu.VMEM(merged.shape, BF16), pltpu.VMEM((rows, columns), F32)]
-        + [pltpu.VMEM(half.shape, F32)] * 2
         + [pltpu.SemaphoreType.DMA((32,))],
         compiler_params=ROW_PARAMS,
         cost_estimate=pl.CostEstimate(flops=3 * 10**9, transcendentals=0, bytes_accessed=8 << 20),
@@ -382,25 +376,11 @@
     )(place, x, merged)
 
 
-def add_halves_kernel(ring, place, keep_ref, got_ref, *refs):
-    outs, (k_buf, g_buf, in_sems, out_sems) = refs[:ring], refs[ring:]
+def add_halves_kernel(ring, place, keep_ref, got_ref, *outs):
     size = outs[0].shape[0]
-    copies = []
-    for d in range(ring):
+    for d, out in enumerate(outs):
         rows = pl.ds(pl.multiple_of(lax.rem(place[0] + d, ring) * size, size), size)
-        copies.append(pltpu.make_async_copy(keep_ref.at[rows], k_buf.at[d], in_sems.at[0, d]))
-        copies.append(pltpu.make_async_copy(got_ref.at[rows], g_buf.at[d], in_sems.at[1, d]))
-    for copy in copies:
-        copy.start()
-    sends = []
-    for d, out in enumerate(outs):
-        copies[2 * d].wait()
-        copies[2 * d + 1].wait()
-        g_buf[d] = g_buf[d] + k_buf[d]
-        sends.append(pltpu.make_async_copy(g_buf.at[d], out, out_sems.at[d]))
-        sends[-1].start()
-    for send in sends:
-        send.wait()
+        out[...] = keep_ref[rows, :] + got_ref[rows, :]
 
 
 def add_halves(keep, got, place, ring):
@@ -410,50 +390,29 @@
     return pl.pallas_call(
         functools.partial(add_halves_kernel, ring),
         out_shape=(piece,) * ring,
-        in_specs=[SMEM0, ANYWHERE, ANYWHERE],
-        out_specs=(ANYWHERE,) * ring,
-        scratch_shapes=[pltpu.VMEM((ring, size, columns), F32)] * 2
-        + [pltpu.SemaphoreType.DMA((2, ring)), pltpu.SemaphoreType.DMA((ring,))],
+        in_specs=[SMEM0, VMEM, VMEM],
+        out_specs=(VMEM,) * ring,
         compiler_params=SUM_PARAMS,
         cost_estimate=pl.CostEstimate(flops=keep.size, transcendentals=0, bytes_accessed=12 * keep.size),
         name="add_halves",
     )(place, keep, got)
 
 
-def add_pieces_kernel(count, *refs):
-    pieces, out = refs[:count], refs[count]
-    buf, in_sems, out_sems = refs[count + 1 :]
-    parts = buf.shape[1]
-    size = out.shape[0] // parts
-    copies = []
-    for p in range(parts):
-        for n, piece in enumerate(pieces):
-            copies.append(pltpu.make_async_copy(piece.at[pl.ds(p * size, size)], buf.at[n, p], in_sems.at[n, p]))
-            copies[-1].start()
-    sends = []
-    for p in range(parts):
-        for n in range(count):
-            copies[p * count + n].wait()
-        total = buf[0, p]
-        for n in range(1, count):
-            total = total + buf[n, p]
-        buf[0, p] = total
-        sends.append(pltpu.make_async_copy(buf.at[0, p], out.at[pl.ds(p * size, size)], out_sems.at[p]))
-        sends[-1].start()
-    for send in sends:
-        send.wait()
+def add_pieces_kernel(*refs):
+    total = refs[0][...]
+    for ref in refs[1:-1]:
+        total = total + ref[...]
+    refs[-1][...] = total
 
 
 def add_pieces(pieces):
     rows, columns = pieces[0].shape
-    count, parts = len(pieces), 2
-    return pl.pallas_call(
-        functools.partial(add_pieces_kernel, count),
+    count = len(pieces)
+    return pl.pallas_call(
+        add_pieces_kernel,
         out_shape=jax.ShapeDtypeStruct((rows, columns), F32),
-        in_specs=[ANYWHERE] * count,
-        out_specs=ANYWHERE,
-        scratch_shapes=[pltpu.VMEM((count, parts, rows // parts, columns), F32)]
-        + [pltpu.SemaphoreType.DMA((count, parts)), pltpu.SemaphoreType.DMA((parts,))],
+        in_specs=[VMEM] * count,
+        out_specs=VMEM,
         compiler_params=SUM_PARAMS,
         cost_estimate=pl.CostEstimate(flops=4 * pieces[0].size, transcendentals=0, bytes_accessed=20 * pieces[0].size),
         name="add_pieces",

time: 227 us -> 220 us (0.969)
  the two profiles are of different devices: /device:TPU:25 before, /device:TPU:0 now
where the time goes in v3:
time: 220 us
  waiting for transfers between devices  107 us (49%)
  Pallas kernels  69 us (31%)
  starting transfers between devices  41.1 us (19%)
    all_to_all x4, waiting for transfers between devices, exchange(): lax.all_to_all(x.reshape(nodes, rows // nodes, columns), 'node', split_ax...  54.6 us
    ppermute x6, waiting for transfers between devices, shards(): mine.append(lax.ppermute(total_piece, 'block', shift[d]))  25.5 us
    ppermute x6, waiting for transfers between devices, shards(): got.append(lax.ppermute(pieces[d], 'block', shift[d]))  23.5 us
    all_to_all x4, starting transfers between devices, exchange(): lax.all_to_all(x.reshape(nodes, rows // nodes, columns), 'node', split_ax...  23.2 us
    pallas_call x3, Pallas kernels, merged_columns(): pl.pallas_call(functools.partial(merged_column_kernel, back, chunk), out_...  19.5 us
    pallas_call x2, Pallas kernels, weigh_back(): pl.pallas_call(functools.partial(weigh_kernel, first_bit, span, ring, chu...  13.8 us
    pallas_call x2, Pallas kernels, row_tree(): pl.pallas_call(functools.partial(row_kernel, first_bit, span), out_shape=...  10.9 us
    ppermute x6, starting transfers between devices, shards(): got.append(lax.ppermute(pieces[d], 'block', shift[d]))  9.23 us
  transfers between devices with their start and end apart: 26, of which 15 were waited for; matrix products, arithmetic and copies ran while one was open for 0% of the time, Pallas kernels for 22%

profile of v3, /device:TPU:0, one launch (start us, length us, event | category | flops | bytes accessed | tf_op | source)
XLA Modules:
  0.0 219.5 jit_solution(13656074083195758808)
XLA Ops:
  0.6 7.4 %column_tree.1 = f32[2048,256]{1,0:T(8,128)} custom-call(s32[5,1,32]{2,1,0:T(1,128)} %bitcast.26, f32[2048,512]{1,0:T(8,128)} %bitcast.23, f32[1,5,32,64,128]{4,3,2,1,0:T(8,128)} %fe_ref.1), custom_call_target="tpu_custom_call" | custom-call | flops 5000000000 | bytes 9437184 | tf_op jit(solution)/shard_map/column_tree/pallas_call | solution.py:112
  8.0 8.1 %all-to-all-start = ((f32[16,128,256]{2,1,0:T(8,128)}), f32[16,128,256]{2,1,0:T(8,128)}, u32[]{:S(2)}, u32[]{:S(2)}) async-start(f32[16,128,256]{2,1,0:T(8,128)} %bitcast.22), calls=%async_computation | async-start | bytes 4194304 | tf_op jit(solution)/shard_map/all_to_all | solution.py:481
  16.1 8.0 %merge_columns.1 = (bf16[16,256,128]{2,1,0:T(8,128)(2,1)}, bf16[16,256,128]{2,1,0:T(8,128)(2,1)}, bf16[2,8,2,256,256]{4,3,2,1,0:T(8,128)(2,1)}, bf16[2,8,2,256,256]{4,3,2,1,0:T(8,128)(2,1)}) custom-call(s32[5,1,32]{2,1,0:T(1,128)} %bitcast.27, f32[1,5,32,64,128]{4,3,2,1,0:T(8,128)} %fe_ref.1, f32[1,5,32,64,128]{4,3,2,1,0:T(8,128)} %fe_ref.1, ...), custom_call_target="tpu_custom_call" | custom-call | flops 10000000000 | bytes 15728640 | tf_op jit(solution)/shard_map/merge_columns/pallas_call | solution.py:216
  24.1 7.4 %merge_rows.1 = (f32[2048,128]{1,0:T(8,128)}, bf16[2,8,2,256,256]{4,3,2,1,0:T(8,128)(2,1)}, bf16[2,8,2,256,256]{4,3,2,1,0:T(8,128)(2,1)}) custom-call(s32[4,1,32]{2,1,0:T(1,128)} %bitcast.28, f32[1,4,32,64,128]{4,3,2,1,0:T(8,128)} %fb_ref.2, f32[1,4,32,64,128]{4,3,2,1,0:T(8,128)} %fb_ref.2, f32[16,128]{1,0:T(8,128)} %bitcast.25), custom_call_target="tpu_custom_call" | custom-call | flops 10000000000 | bytes 12582912 | tf_op jit(solution)/shard_map/merge_rows/pallas_call | solution.py:233
  31.5 6.5 %column_tree_merged.1 = f32[2048,256]{1,0:T(8,128)} custom-call(f32[2048,512]{1,0:T(8,128)} %bitcast.24, bf16[16,256,128]{2,1,0:T(8,128)(2,1)} %get-tuple-element.39.w_ref, bf16[2,8,2,256,256]{4,3,2,1,0:T(8,128)(2,1)} %get-tuple-element.40.g_ref, f32[2048,128]{1,0:T(8,128)} %get-tuple-element.41.rest_0_.refs_8_), custom_call_target="tpu_custom_call" | custom-call | flops 4000000000 | bytes 9437184 | tf_op jit(solution)/shard_map/column_tree_merged/pallas_call | solution.py:323
  38.0 8.5 %all-to-all-done = f32[16,128,256]{2,1,0:T(8,128)} async-done(((f32[16,128,256]{2,1,0:T(8,128)}), f32[16,128,256]{2,1,0:T(8,128)}, u32[]{:S(2)}, u32[]{:S(2)}) %all-to-all-start) | async-done | bytes 2097184 | tf_op jit(solution)/shard_map/all_to_all | solution.py:481
  46.5 3.9 %all-to-all-start.1 = ((f32[16,128,256]{2,1,0:T(8,128)}), f32[16,128,256]{2,1,0:T(8,128)S(1)}, u32[]{:S(2)}, u32[]{:S(2)}) async-start(f32[16,128,256]{2,1,0:T(8,128)} %bitcast.20), calls=%async_computation.1 | async-start | bytes 4194304 | tf_op jit(solution)/shard_map/all_to_all | solution.py:481
  50.5 6.0 %row_tree.2 = (f32[1024,256]{1,0:T(8,128)S(1)}, f32[1024,256]{1,0:T(8,128)}) custom-call(s32[2]{0:T(128)S(1)} %pad_add_fusion.place, f32[2048,256]{1,0:T(8,128)} %bitcast.5.x_ref, bf16[2,8,2,256,256]{4,3,2,1,0:T(8,128)(2,1)} %get-tuple-element.32.g_ref), custom_call_target="tpu_custom_call" | custom-call | flops 3000000000 | bytes 8388608 | tf_op jit(solution)/shard_map/row_tree/pallas_call | solution.py:366
  56.7 21.3 %all-to-all-done.1 = f32[16,128,256]{2,1,0:T(8,128)S(1)} async-done(((f32[16,128,256]{2,1,0:T(8,128)}), f32[16,128,256]{2,1,0:T(8,128)S(1)}, u32[]{:S(2)}, u32[]{:S(2)}) %all-to-all-start.1) | async-done | bytes 2097184 | tf_op jit(solution)/shard_map/all_to_all | solution.py:481
  77.9 4.9 %row_tree.3 = (f32[1024,256]{1,0:T(8,128)S(1)}, f32[1024,256]{1,0:T(8,128)S(1)}) custom-call(s32[2]{0:T(128)S(1)} %pad_add_fusion.place, f32[2048,256]{1,0:T(8,128)S(1)} %bitcast.17, bf16[2,8,2,256,256]{4,3,2,1,0:T(8,128)(2,1)} %get-tuple-element.32.g_ref), custom_call_target="tpu_custom_call" | custom-call | flops 3000000000 | bytes 8388608 | tf_op jit(solution)/shard_map/row_tree/pallas_call | solution.py:366
  83.0 1.4 add_halves.2
  84.3 1.7 collective-permute-start.1
  86.0 2.9 %collective-permute-start.2 = (f32[256,256]{1,0:T(8,128)S(1)}, f32[256,256]{1,0:T(8,128)S(1)}, u32[]{:S(2)}, u32[]{:S(2)}) collective-permute-start(f32[256,256]{1,0:T(8,128)S(1)} %get-tuple-element.37), channel_id=1, source_target_pairs={{0,64},{16,80},{32,96},{48,112},{64,0},{80,16},{96,32},{112,48},{1... | collective-permute-start | bytes 786440 | tf_op jit(solution)/shard_map/ppermute | solution.py:521
  88.9 1.3 collective-permute-start.3
  90.3 4.1 %collective-permute-done.1.refs_1_ = f32[256,256]{1,0:T(8,128)S(1)} collective-permute-done((f32[256,256]{1,0:T(8,128)S(1)}, f32[256,256]{1,0:T(8,128)S(1)}, u32[]{:S(2)}, u32[]{:S(2)}) %collective-permute-start.1) | collective-permute-done | bytes 262176 | tf_op jit(solution)/shard_map/ppermute | solution.py:521
  94.4 6.8 %collective-permute-done.2.refs_2_ = f32[256,256]{1,0:T(8,128)S(1)} collective-permute-done((f32[256,256]{1,0:T(8,128)S(1)}, f32[256,256]{1,0:T(8,128)S(1)}, u32[]{:S(2)}, u32[]{:S(2)}) %collective-permute-start.2) | collective-permute-done | bytes 262176 | tf_op jit(solution)/shard_map/ppermute | solution.py:521
  101.3 2.2 %collective-permute-start.6 = (f32[256,256]{1,0:T(8,128)S(1)}, f32[256,256]{1,0:T(8,128)S(1)}, u32[]{:S(2)}, u32[]{:S(2)}) collective-permute-start(f32[256,256]{1,0:T(8,128)S(1)} %add_pieces.2.refs_0_), channel_id=1, source_target_pairs={{0,96},{16,112},{32,0},{48,16},{64,32},{80,48},{96,64},{112,80},{1... | collective-permute-start | bytes 786440 | tf_op jit(solution)/shard_map/ppermute | solution.py:525
  106.1 8.8 %collective-permute-done.6.refs_3_ = f32[256,256]{1,0:T(8,128)S(1)} collective-permute-done((f32[256,256]{1,0:T(8,128)S(1)}, f32[256,256]{1,0:T(8,128)S(1)}, u32[]{:S(2)}, u32[]{:S(2)}) %collective-permute-start.6) | collective-permute-done | bytes 262176 | tf_op jit(solution)/shard_map/ppermute | solution.py:525
  114.9 3.5 %collective-permute-done.4.refs_1_ = f32[256,256]{1,0:T(8,128)S(1)} collective-permute-done((f32[256,256]{1,0:T(8,128)S(1)}, f32[256,256]{1,0:T(8,128)S(1)}, u32[]{:S(2)}, u32[]{:S(2)}) %collective-permute-start.4) | collective-permute-done | bytes 262176 | tf_op jit(solution)/shard_map/ppermute | solution.py:525
  121.4 6.9 %weigh_back.2 = (f32[2048,512]{1,0:T(8,128)}, f32[2048,256]{1,0:T(8,128)}) custom-call(s32[2]{0:T(128)} %copy-done.2, f32[256,256]{1,0:T(8,128)} %copy-done.1, f32[256,256]{1,0:T(8,128)} %copy-done.12, f32[256,256]{1,0:T(8,128)} %copy-done.11, f32[256,256]{1,0:T(8,128)} %copy-done.10, f32[256,256]{1,0:T(8,128)} %copy-done.13, f32[256,256]{1,0:T(8,128)} %copy-done.14, ...), custom_call_target="tpu_custom_call" | custom-call | flops 3000000000 | bytes 12582912 | tf_op jit(solution)/shard_map/weigh_back/pallas_call | solution.py:463
  128.3 4.5 %all-to-all-start.3 = ((f32[16,128,256]{2,1,0:T(8,128)}), f32[16,128,256]{2,1,0:T(8,128)}, u32[]{:S(2)}, u32[]{:S(2)}) async-start(f32[16,128,256]{2,1,0:T(8,128)} %bitcast.19), calls=%async_computation.3 | async-start | bytes 4194304 | tf_op jit(solution)/shard_map/all_to_all | solution.py:481
  132.8 2.2 collective-permute-start.9
  136.1 11.9 %collective-permute-done.8.refs_1_ = f32[256,256]{1,0:T(8,128)S(1)} collective-permute-done((f32[256,256]{1,0:T(8,128)S(1)}, f32[256,256]{1,0:T(8,128)S(1)}, u32[]{:S(2)}, u32[]{:S(2)}) %collective-permute-start.8) | collective-permute-done | bytes 262176 | tf_op jit(solution)/shard_map/ppermute | solution.py:521
  148.7 2.4 %collective-permute-start.13 = (f32[256,256]{1,0:T(8,128)S(1)}, f32[256,256]{1,0:T(8,128)S(1)}, u32[]{:S(2)}, u32[]{:S(2)}) collective-permute-start(f32[256,256]{1,0:T(8,128)S(1)} %add_pieces.3.refs_0_), channel_id=1, source_target_pairs={{0,96},{16,112},{32,0},{48,16},{64,32},{80,48},{96,64},{112,80},{1... | collective-permute-start | bytes 786440 | tf_op jit(solution)/shard_map/ppermute | solution.py:525
  152.1 10.2 %collective-permute-done.13.refs_3_ = f32[256,256]{1,0:T(8,128)S(1)} collective-permute-done((f32[256,256]{1,0:T(8,128)S(1)}, f32[256,256]{1,0:T(8,128)S(1)}, u32[]{:S(2)}, u32[]{:S(2)}) %collective-permute-start.13) | collective-permute-done | bytes 262176 | tf_op jit(solution)/shard_map/ppermute | solution.py:525
  162.8 2.9 %collective-permute-done.11.refs_1_ = f32[256,256]{1,0:T(8,128)S(1)} collective-permute-done((f32[256,256]{1,0:T(8,128)S(1)}, f32[256,256]{1,0:T(8,128)S(1)}, u32[]{:S(2)}, u32[]{:S(2)}) %collective-permute-start.11) | collective-permute-done | bytes 262176 | tf_op jit(solution)/shard_map/ppermute | solution.py:525
  165.8 1.5 collective-permute-done.15.refs_5_
  168.0 6.9 %weigh_back.3 = (f32[2048,512]{1,0:T(8,128)}, f32[2048,256]{1,0:T(8,128)}) custom-call(s32[2]{0:T(128)} %copy-done.2, f32[256,256]{1,0:T(8,128)} %copy-done, f32[256,256]{1,0:T(8,128)} %copy-done.5, f32[256,256]{1,0:T(8,128)} %copy-done.4, f32[256,256]{1,0:T(8,128)} %copy-done.3, f32[256,256]{1,0:T(8,128)} %copy-done.6, ...), custom_call_target="tpu_custom_call", output_to_operand_aliasing={{0}: (11, {})} | custom-call | flops 3000000000 | bytes 12582912 | tf_op jit(solution)/shard_map/weigh_back/pallas_call | solution.py:463
  174.9 6.8 %all-to-all-start.2 = ((f32[16,128,256]{2,1,0:T(8,128)}), f32[16,128,256]{2,1,0:T(8,128)}, u32[]{:S(2)}, u32[]{:S(2)}) async-start(f32[16,128,256]{2,1,0:T(8,128)} %bitcast.21), calls=%async_computation.2 | async-start | bytes 4194304 | tf_op jit(solution)/shard_map/all_to_all | solution.py:481
  181.7 6.5 %column_back.2.rest_0_ = f32[2048,512]{1,0:T(8,128)} custom-call(f32[2048,256]{1,0:T(8,128)} %bitcast.14.x_ref, bf16[16,256,128]{2,1,0:T(8,128)(2,1)} %get-tuple-element.59.w_ref, bf16[2,8,2,256,256]{4,3,2,1,0:T(8,128)(2,1)} %get-tuple-element.60.g_ref), custom_call_target="tpu_custom_call" | custom-call | flops 4000000000 | bytes 9437184 | tf_op jit(solution)/shard_map/column_back/pallas_call | solution.py:323
  188.1 24.7 %all-to-all-done.2 = f32[16,128,256]{2,1,0:T(8,128)} async-done(((f32[16,128,256]{2,1,0:T(8,128)}), f32[16,128,256]{2,1,0:T(8,128)}, u32[]{:S(2)}, u32[]{:S(2)}) %all-to-all-start.2) | async-done | bytes 2097184 | tf_op jit(solution)/shard_map/all_to_all | solution.py:481
  212.9 6.5 %column_back.3 = f32[2048,512]{1,0:T(8,128)} custom-call(f32[2048,256]{1,0:T(8,128)} %bitcast.12.x_ref, bf16[16,256,128]{2,1,0:T(8,128)(2,1)} %get-tuple-element.59.w_ref, bf16[2,8,2,256,256]{4,3,2,1,0:T(8,128)(2,1)} %get-tuple-element.60.g_ref, f32[2048,512]{1,0:T(8,128)} %column_back.2.rest_0_), custom_call_target="tpu_custom_call", output_to_operand_aliasing={{}: (3, {})} | custom-call | flops 4000000000 | bytes 9437184 | tf_op jit(solution)/shard_map/column_back/pallas_call | solution.py:323
  (69 shorter events, 9.8 us)
Async XLA Ops:
  8.0 38.5 %all-to-all-start = ((f32[16,128,256]{2,1,0:T(8,128)}), f32[16,128,256]{2,1,0:T(8,128)}, u32[]{:S(2)}, u32[]{:S(2)}) async-start(f32[16,128,256]{2,1,0:T(8,128)} %bitcast.22), calls=%async_computation | async-start | bytes 4194304 | tf_op jit(solution)/shard_map/all_to_all | solution.py:481
  46.5 31.4 %all-to-all-start.1 = ((f32[16,128,256]{2,1,0:T(8,128)}), f32[16,128,256]{2,1,0:T(8,128)S(1)}, u32[]{:S(2)}, u32[]{:S(2)}) async-start(f32[16,128,256]{2,1,0:T(8,128)} %bitcast.20), calls=%async_computation.1 | async-start | bytes 4194304 | tf_op jit(solution)/shard_map/all_to_all | solution.py:481
  50.5 54.8 %copy-start.2 = (s32[2]{0:T(128)}, s32[2]{0:T(128)S(1)}, u32[]{:S(2)}) copy-start(s32[2]{0:T(128)S(1)} %pad_add_fusion.place) | copy-start | bytes 28
  56.6 26.4 %collective-permute-start = (f32[1024,256]{1,0:T(8,128)}, f32[1024,256]{1,0:T(8,128)}, u32[]{:S(2)}, u32[]{:S(2)}) collective-permute-start(f32[1024,256]{1,0:T(8,128)} %get-tuple-element.34), channel_id=1, source_target_pairs={{0,16},{16,0},{32,48},{48,32},{64,80},{80,64},{96,112},{112,96},{1... | collective-permute-start | bytes 3145736 | tf_op jit(solution)/shard_map/ppermute | solution.py:511
  82.9 22.5 %collective-permute-start.7 = (f32[1024,256]{1,0:T(8,128)S(1)}, f32[1024,256]{1,0:T(8,128)S(1)}, u32[]{:S(2)}, u32[]{:S(2)}) collective-permute-start(f32[1024,256]{1,0:T(8,128)S(1)} %get-tuple-element.43), channel_id=1, source_target_pairs={{0,16},{16,0},{32,48},{48,32},{64,80},{80,64},{96,112},{112,96},{1... | collective-permute-start | bytes 3145736 | tf_op jit(solution)/shard_map/ppermute | solution.py:511
  84.3 10.1 %collective-permute-start.1 = (f32[256,256]{1,0:T(8,128)S(1)}, f32[256,256]{1,0:T(8,128)S(1)}, u32[]{:S(2)}, u32[]{:S(2)}) collective-permute-start(f32[256,256]{1,0:T(8,128)S(1)} %get-tuple-element.36), channel_id=1, source_target_pairs={{0,32},{16,48},{32,64},{48,80},{64,96},{80,112},{96,0},{112,16},{1... | collective-permute-start | bytes 786440 | tf_op jit(solution)/shard_map/ppermute | solution.py:521
  86.0 15.2 %collective-permute-start.2 = (f32[256,256]{1,0:T(8,128)S(1)}, f32[256,256]{1,0:T(8,128)S(1)}, u32[]{:S(2)}, u32[]{:S(2)}) collective-permute-start(f32[256,256]{1,0:T(8,128)S(1)} %get-tuple-element.37), channel_id=1, source_target_pairs={{0,64},{16,80},{32,96},{48,112},{64,0},{80,16},{96,32},{112,48},{1... | collective-permute-start | bytes 786440 | tf_op jit(solution)/shard_map/ppermute | solution.py:521
  88.9 12.3 %collective-permute-start.3 = (f32[256,256]{1,0:T(8,128)S(1)}, f32[256,256]{1,0:T(8,128)S(1)}, u32[]{:S(2)}, u32[]{:S(2)}) collective-permute-start(f32[256,256]{1,0:T(8,128)S(1)} %get-tuple-element.38), channel_id=1, source_target_pairs={{0,96},{16,112},{32,0},{48,16},{64,32},{80,48},{96,64},{112,80},{1... | collective-permute-start | bytes 786440 | tf_op jit(solution)/shard_map/ppermute | solution.py:521
  101.3 19.5 %copy-start.1 = (f32[256,256]{1,0:T(8,128)}, f32[256,256]{1,0:T(8,128)S(1)}, u32[]{:S(2)}) copy-start(f32[256,256]{1,0:T(8,128)S(1)} %add_pieces.2.refs_0_) | copy-start | bytes 786436
  101.3 13.6 %collective-permute-start.6 = (f32[256,256]{1,0:T(8,128)S(1)}, f32[256,256]{1,0:T(8,128)S(1)}, u32[]{:S(2)}, u32[]{:S(2)}) collective-permute-start(f32[256,256]{1,0:T(8,128)S(1)} %add_pieces.2.refs_0_), channel_id=1, source_target_pairs={{0,96},{16,112},{32,0},{48,16},{64,32},{80,48},{96,64},{112,80},{1... | collective-permute-start | bytes 786440 | tf_op jit(solution)/shard_map/ppermute | solution.py:525
  103.5 11.4 %collective-permute-start.5 = (f32[256,256]{1,0:T(8,128)S(1)}, f32[256,256]{1,0:T(8,128)S(1)}, u32[]{:S(2)}, u32[]{:S(2)}) collective-permute-start(f32[256,256]{1,0:T(8,128)S(1)} %add_pieces.2.refs_0_), channel_id=1, source_target_pairs={{0,64},{16,80},{32,96},{48,112},{64,0},{80,16},{96,32},{112,48},{1... | collective-permute-start | bytes 786440 | tf_op jit(solution)/shard_map/ppermute | solution.py:525
  104.6 13.8 %collective-permute-start.4 = (f32[256,256]{1,0:T(8,128)S(1)}, f32[256,256]{1,0:T(8,128)S(1)}, u32[]{:S(2)}, u32[]{:S(2)}) collective-permute-start(f32[256,256]{1,0:T(8,128)S(1)} %add_pieces.2.refs_0_), channel_id=1, source_target_pairs={{0,32},{16,48},{32,64},{48,80},{64,96},{80,112},{96,0},{112,16},{1... | collective-permute-start | bytes 786440 | tf_op jit(solution)/shard_map/ppermute | solution.py:525
  106.0 13.0 %collective-permute-start.18 = (f32[256,256]{1,0:T(8,128)S(1)}, f32[256,256]{1,0:T(8,128)S(1)}, u32[]{:S(2)}, u32[]{:S(2)}) collective-permute-start(f32[256,256]{1,0:T(8,128)S(1)} %add_pieces.2.refs_0_), channel_id=1, source_target_pairs={{0,16},{16,0},{32,48},{48,32},{64,80},{80,64},{96,112},{112,96},{1... | collective-permute-start | bytes 786440 | tf_op jit(solution)/shard_map/ppermute | solution.py:529
  114.9 5.8 %copy-start.10 = (f32[256,256]{1,0:T(8,128)}, f32[256,256]{1,0:T(8,128)S(1)}, u32[]{:S(2)}) copy-start(f32[256,256]{1,0:T(8,128)S(1)} %collective-permute-done.6.refs_3_) | copy-start | bytes 786436
  114.9 5.8 %copy-start.11 = (f32[256,256]{1,0:T(8,128)}, f32[256,256]{1,0:T(8,128)S(1)}, u32[]{:S(2)}) copy-start(f32[256,256]{1,0:T(8,128)S(1)} %collective-permute-done.5.refs_2_) | copy-start | bytes 786436
  118.4 1.5 collective-permute-start.19
  118.4 1.9 collective-permute-start.20
  118.9 1.8 collective-permute-start.21
  128.3 46.6 %all-to-all-start.3 = ((f32[16,128,256]{2,1,0:T(8,128)}), f32[16,128,256]{2,1,0:T(8,128)}, u32[]{:S(2)}, u32[]{:S(2)}) async-start(f32[16,128,256]{2,1,0:T(8,128)} %bitcast.19), calls=%async_computation.3 | async-start | bytes 4194304 | tf_op jit(solution)/shard_map/all_to_all | solution.py:481
  132.8 15.2 %collective-permute-start.8 = (f32[256,256]{1,0:T(8,128)S(1)}, f32[256,256]{1,0:T(8,128)S(1)}, u32[]{:S(2)}, u32[]{:S(2)}) collective-permute-start(f32[256,256]{1,0:T(8,128)S(1)} %get-tuple-element.49), channel_id=1, source_target_pairs={{0,32},{16,48},{32,64},{48,80},{64,96},{80,112},{96,0},{112,16},{1... | collective-permute-start | bytes 786440 | tf_op jit(solution)/shard_map/ppermute | solution.py:521
  132.8 15.2 %collective-permute-start.9 = (f32[256,256]{1,0:T(8,128)S(1)}, f32[256,256]{1,0:T(8,128)S(1)}, u32[]{:S(2)}, u32[]{:S(2)}) collective-permute-start(f32[256,256]{1,0:T(8,128)S(1)} %get-tuple-element.50), channel_id=1, source_target_pairs={{0,64},{16,80},{32,96},{48,112},{64,0},{80,16},{96,32},{112,48},{1... | collective-permute-start | bytes 786440 | tf_op jit(solution)/shard_map/ppermute | solution.py:521
  135.0 13.6 %collective-permute-start.10 = (f32[256,256]{1,0:T(8,128)S(1)}, f32[256,256]{1,0:T(8,128)S(1)}, u32[]{:S(2)}, u32[]{:S(2)}) collective-permute-start(f32[256,256]{1,0:T(8,128)S(1)} %get-tuple-element.51), channel_id=1, source_target_pairs={{0,96},{16,112},{32,0},{48,16},{64,32},{80,48},{96,64},{112,80},{1... | collective-permute-start | bytes 786440 | tf_op jit(solution)/shard_map/ppermute | solution.py:521
  148.7 18.6 %copy-start = (f32[256,256]{1,0:T(8,128)}, f32[256,256]{1,0:T(8,128)S(1)}, u32[]{:S(2)}) copy-start(f32[256,256]{1,0:T(8,128)S(1)} %add_pieces.3.refs_0_) | copy-start | bytes 786436
  148.7 13.6 %collective-permute-start.13 = (f32[256,256]{1,0:T(8,128)S(1)}, f32[256,256]{1,0:T(8,128)S(1)}, u32[]{:S(2)}, u32[]{:S(2)}) collective-permute-start(f32[256,256]{1,0:T(8,128)S(1)} %add_pieces.3.refs_0_), channel_id=1, source_target_pairs={{0,96},{16,112},{32,0},{48,16},{64,32},{80,48},{96,64},{112,80},{1... | collective-permute-start | bytes 786440 | tf_op jit(solution)/shard_map/ppermute | solution.py:525
  151.1 11.2 %collective-permute-start.12 = (f32[256,256]{1,0:T(8,128)S(1)}, f32[256,256]{1,0:T(8,128)S(1)}, u32[]{:S(2)}, u32[]{:S(2)}) collective-permute-start(f32[256,256]{1,0:T(8,128)S(1)} %add_pieces.3.refs_0_), channel_id=1, source_target_pairs={{0,64},{16,80},{32,96},{48,112},{64,0},{80,16},{96,32},{112,48},{1... | collective-permute-start | bytes 786440 | tf_op jit(solution)/shard_map/ppermute | solution.py:525
  151.1 14.6 %collective-permute-start.11 = (f32[256,256]{1,0:T(8,128)S(1)}, f32[256,256]{1,0:T(8,128)S(1)}, u32[]{:S(2)}, u32[]{:S(2)}) collective-permute-start(f32[256,256]{1,0:T(8,128)S(1)} %add_pieces.3.refs_0_), channel_id=1, source_target_pairs={{0,32},{16,48},{32,64},{48,80},{64,96},{80,112},{96,0},{112,16},{1... | collective-permute-start | bytes 786440 | tf_op jit(solution)/shard_map/ppermute | solution.py:525
  152.1 13.7 %collective-permute-start.14 = (f32[256,256]{1,0:T(8,128)S(1)}, f32[256,256]{1,0:T(8,128)S(1)}, u32[]{:S(2)}, u32[]{:S(2)}) collective-permute-start(f32[256,256]{1,0:T(8,128)S(1)} %add_pieces.3.refs_0_), channel_id=1, source_target_pairs={{0,16},{16,0},{32,48},{48,32},{64,80},{80,64},{96,112},{112,96},{1... | collective-permute-start | bytes 786440 | tf_op jit(solution)/shard_map/ppermute | solution.py:529
  162.3 5.0 %copy-start.3 = (f32[256,256]{1,0:T(8,128)}, f32[256,256]{1,0:T(8,128)S(1)}, u32[]{:S(2)}) copy-start(f32[256,256]{1,0:T(8,128)S(1)} %collective-permute-done.13.refs_3_) | copy-start | bytes 786436
  162.3 3.4 %collective-permute-start.17 = (f32[256,256]{1,0:T(8,128)S(1)}, f32[256,256]{1,0:T(8,128)S(1)}, u32[]{:S(2)}, u32[]{:S(2)}) collective-permute-start(f32[256,256]{1,0:T(8,128)S(1)} %collective-permute-done.13.refs_3_), channel_id=1, source_target_pairs={{0,16},{16,0},{32,48},{48,32},{64,80},{80,64},{96,112},{112,96},{1... | collective-permute-start | bytes 786440 | tf_op jit(solution)/shard_map/ppermute | solution.py:529
  162.3 3.4 %collective-permute-start.16 = (f32[256,256]{1,0:T(8,128)S(1)}, f32[256,256]{1,0:T(8,128)S(1)}, u32[]{:S(2)}, u32[]{:S(2)}) collective-permute-start(f32[256,256]{1,0:T(8,128)S(1)} %collective-permute-done.12.refs_2_), channel_id=1, source_target_pairs={{0,16},{16,0},{32,48},{48,32},{64,80},{80,64},{96,112},{112,96},{1... | collective-permute-start | bytes 786440 | tf_op jit(solution)/shard_map/ppermute | solution.py:529
  165.7 1.5 collective-permute-start.15
  174.9 38.0 %all-to-all-start.2 = ((f32[16,128,256]{2,1,0:T(8,128)}), f32[16,128,256]{2,1,0:T(8,128)}, u32[]{:S(2)}, u32[]{:S(2)}) async-start(f32[16,128,256]{2,1,0:T(8,128)} %bitcast.21), calls=%async_computation.2 | async-start | bytes 4194304 | tf_op jit(solution)/shard_map/all_to_all | solution.py:481
  (11 other events, 18.2 us)
